TPU v7x, 512 devices: a whole 4x4x16 slice. The times are simulated.
512 devices in a mesh: ctx: 64 (over z_hi, x, y, core), kvh: 8 (over z_lo).
Axes of the slice: x: 4, y: 4, z: 16 (z_hi: 2, z_lo: 8; z = z_hi * 8 + z_lo), core: 2. Of those that a mesh axis runs over, the one named last changes fastest.
Arguments:
- doc_lengths: int32 [33], replicated, may hold values from 1 to 896, 16384 in all
- queries: bfloat16 [16384, 4096], P('ctx', 'kvh'), may hold values from -6 to 6
- keys: bfloat16 [16384, 1024], P('ctx', 'kvh'), may hold values from -6 to 6
- values: bfloat16 [16384, 1024], P('ctx', 'kvh'), may hold values from -12 to 12
- o_weight: bfloat16 [4096, 4096], P('kvh'), may hold values from -0.09375 to 0.09375
Outputs:
- projected: bfloat16 [16384, 4096], P(('ctx', 'kvh'))
Inputs may be any that keep to these rules, and one draw needn't show every extreme that they name: `doc_lengths`: the documents in sequence order; they sum to 16384.
All inputs are finite; a program needn't handle non-finite values.
Results may differ from a plain program's by a relative error of at most 0.018.
Values may be sent and summed in bfloat16 or wider, within the bound.
No kernel may reach another device: no remote copies, remote signals or barrier semaphores. Data moves between devices by JAX's collectives and lax.ppermute only.
A program may use at most 64 MiB of HBM per device.

v0:
```python
import math

import jax
import jax.numpy as jnp
from jax import lax
from jax.sharding import PartitionSpec as P

HEAD_WIDTH = 128
DOC_STRETCHES = 7


NEG_FILL = -1e30


def from_behind(value, axis, steps):
    count = lax.axis_size(axis)
    initial, last = (max(0, -steps), min(count, count - steps))
    return lax.ppermute(value, axis, [(source, source + steps) for source in range(initial, last)])


def local(doc_lengths, queries, keys, values, o_weight):
    rows_dev = queries.shape[0]
    half_rows = rows_dev // 2
    ctx_count = lax.axis_size("ctx")
    ctx_index = lax.axis_index("ctx")
    seq_total = ctx_count * rows_dev
    doc_ends = jnp.cumsum(doc_lengths)
    offset_rows = jnp.arange(rows_dev, dtype=jnp.int32)
    scaling = 1.0 / math.sqrt(HEAD_WIDTH)

    def block_places(source_index):
        return jnp.where(
            offset_rows < half_rows,
            source_index * half_rows + offset_rows,
            seq_total - (source_index + 2) * half_rows + offset_rows,
        )

    def document_of(places):
        return jnp.sum((doc_ends[None, :] <= places[:, None]).astype(jnp.int32), axis=1)

    def source_valid(source_index):
        return (source_index >= 0) & (source_index < ctx_count)

    own_places = block_places(ctx_index)
    own_docs = document_of(own_places)
    query_heads = queries.reshape(rows_dev, queries.shape[1] // HEAD_WIDTH, HEAD_WIDTH)
    head_count = query_heads.shape[1]
    stacked = jnp.stack([keys, values])
    blocks = [(stacked, own_places, source_valid(ctx_index))]
    for offset_step in range(1, DOC_STRETCHES + 1):
        blocks.append(
            (
                from_behind(stacked, "ctx", offset_step),
                block_places(ctx_index - offset_step),
                source_valid(ctx_index - offset_step),
            )
        )
        blocks.append(
            (
                from_behind(stacked, "ctx", -offset_step),
                block_places(ctx_index + offset_step),
                source_valid(ctx_index + offset_step),
            )
        )
    merged = (
        jnp.full((rows_dev, head_count), NEG_FILL, jnp.float32),
        jnp.zeros((rows_dev, head_count), jnp.float32),
        jnp.zeros((rows_dev, head_count, HEAD_WIDTH), jnp.float32),
    )
    for key_pair, places, present in blocks:
        allowed = (
            (document_of(places)[None, :] == own_docs[:, None])
            & (places[None, :] <= own_places[:, None])
            & present
        )

        def update(current):
            run_max, run_sum, run_out = current
            scores = (
                jnp.einsum(
                    "cgd,kd->cgk", query_heads, key_pair[0], preferred_element_type=jnp.float32
                )
                * scaling
            )
            scores = jnp.where(allowed[:, None, :], scores, NEG_FILL)
            new_max = jnp.maximum(run_max, jnp.max(scores, axis=2))
            weights = jnp.where(allowed[:, None, :], jnp.exp(scores - new_max[:, :, None]), 0.0)
            factor = jnp.exp(run_max - new_max)
            new_sum = run_sum * factor + jnp.sum(weights, axis=2)
            new_out = run_out * factor[:, :, None] + jnp.einsum(
                "cgk,kd->cgd",
                weights.astype(jnp.bfloat16),
                key_pair[1],
                preferred_element_type=jnp.float32,
            )
            return (new_max, new_sum, new_out)

        merged = lax.cond(jnp.any(allowed), update, lambda current: current, merged)
    attention = (
        (merged[2] / merged[1][:, :, None])
        .reshape(rows_dev, head_count * HEAD_WIDTH)
        .astype(jnp.bfloat16)
    )
    return lax.psum_scatter(
        jnp.dot(attention, o_weight, preferred_element_type=jnp.float32).astype(jnp.bfloat16),
        "kvh",
        scatter_dimension=0,
        tiled=True,
    )


def solution(mesh):
    in_specs = (P(), P("ctx", "kvh"), P("ctx", "kvh"), P("ctx", "kvh"), P("kvh", None))
    out_specs = P(("ctx", "kvh"), None)
    return jax.shard_map(local, mesh=mesh, in_specs=in_specs, out_specs=out_specs, check_vma=False)
```

profile of v0, /device:TPU:6, one launch (start us, length us, event | category | flops | bytes accessed | tf_op | source)
XLA Modules:
  0.0 262.2 jit_solution(9004103881395406695)
XLA Ops:
  6.5 1.5 pad_maximum_fusion
  8.1 1.9 collective-permute-start
  10.0 5.8 %collective-permute-start.1 = (bf16[2,256,128]{2,1,0:T(8,128)(2,1)}, bf16[2,256,128]{2,1,0:T(8,128)(2,1)S(1)}, u32[]{:S(2)}, u32[]{:S(2)}) collective-permute-start(bf16[2,256,128]{2,1,0:T(8,128)(2,1)} %pad_maximum_fusion), channel_id=1, source_target_pairs={{8,0},{16,8},{24,16},{32,24},{40,32},{48,40},{56,48},{64,56},{72,6... | collective-permute-start | bytes 393224 | tf_op jit(solution)/shard_map/ppermute | solution.py:18
  15.8 1.9 collective-permute-start.2
  17.7 6.0 %collective-permute-start.3 = (bf16[2,256,128]{2,1,0:T(8,128)(2,1)}, bf16[2,256,128]{2,1,0:T(8,128)(2,1)S(1)}, u32[]{:S(2)}, u32[]{:S(2)}) collective-permute-start(bf16[2,256,128]{2,1,0:T(8,128)(2,1)} %pad_maximum_fusion), channel_id=1, source_target_pairs={{16,0},{24,8},{32,16},{40,24},{48,32},{56,40},{64,48},{72,56},{80,... | collective-permute-start | bytes 393224 | tf_op jit(solution)/shard_map/ppermute | solution.py:18
  23.7 1.9 collective-permute-start.4
  25.7 0.8 copy.70
  26.7 1.1 copy.71
  28.1 1.4 and_and_fusion
  30.2 6.0 %collective-permute-start.5 = (bf16[2,256,128]{2,1,0:T(8,128)(2,1)}, bf16[2,256,128]{2,1,0:T(8,128)(2,1)S(1)}, u32[]{:S(2)}, u32[]{:S(2)}) collective-permute-start(bf16[2,256,128]{2,1,0:T(8,128)(2,1)} %pad_maximum_fusion), channel_id=1, source_target_pairs={{24,0},{32,8},{40,16},{48,24},{56,32},{64,40},{72,48},{80,56},{88,... | collective-permute-start | bytes 393224 | tf_op jit(solution)/shard_map/ppermute | solution.py:18
  36.2 8.8 %collective-permute-start.6 = (bf16[2,256,128]{2,1,0:T(8,128)(2,1)}, bf16[2,256,128]{2,1,0:T(8,128)(2,1)S(1)}, u32[]{:S(2)}, u32[]{:S(2)}) collective-permute-start(bf16[2,256,128]{2,1,0:T(8,128)(2,1)} %pad_maximum_fusion), channel_id=1, source_target_pairs={{0,32},{8,40},{16,48},{24,56},{32,64},{40,72},{48,80},{56,88},{64,... | collective-permute-start | bytes 393224 | tf_op jit(solution)/shard_map/ppermute | solution.py:18
  45.1 1.9 collective-permute-start.7
  47.0 31.9 %collective-permute-start.8 = (bf16[2,256,128]{2,1,0:T(8,128)(2,1)}, bf16[2,256,128]{2,1,0:T(8,128)(2,1)S(1)}, u32[]{:S(2)}, u32[]{:S(2)}) collective-permute-start(bf16[2,256,128]{2,1,0:T(8,128)(2,1)} %pad_maximum_fusion), channel_id=1, source_target_pairs={{0,40},{8,48},{16,56},{24,64},{32,72},{40,80},{48,88},{56,96},{64,... | collective-permute-start | bytes 393224 | tf_op jit(solution)/shard_map/ppermute | solution.py:18
  78.9 1.3 fusion.180
  80.8 1.9 collective-permute-start.9
  82.8 14.8 %collective-permute-start.10 = (bf16[2,256,128]{2,1,0:T(8,128)(2,1)}, bf16[2,256,128]{2,1,0:T(8,128)(2,1)S(1)}, u32[]{:S(2)}, u32[]{:S(2)}) collective-permute-start(bf16[2,256,128]{2,1,0:T(8,128)(2,1)} %pad_maximum_fusion), channel_id=1, source_target_pairs={{0,48},{8,56},{16,64},{24,72},{32,80},{40,88},{48,96},{56,104},{64... | collective-permute-start | bytes 393224 | tf_op jit(solution)/shard_map/ppermute | solution.py:18
  97.6 1.9 collective-permute-start.11
  99.5 16.5 %collective-permute-start.12 = (bf16[2,256,128]{2,1,0:T(8,128)(2,1)}, bf16[2,256,128]{2,1,0:T(8,128)(2,1)S(1)}, u32[]{:S(2)}, u32[]{:S(2)}) collective-permute-start(bf16[2,256,128]{2,1,0:T(8,128)(2,1)} %pad_maximum_fusion), channel_id=1, source_target_pairs={{0,56},{8,64},{16,72},{24,80},{32,88},{40,96},{48,104},{56,112},{6... | collective-permute-start | bytes 393224 | tf_op jit(solution)/shard_map/ppermute | solution.py:18
  116.1 1.9 collective-permute-start.13
  118.0 1.2 fusion.181
  127.2 4.6 %conditional.15 = (f32[256,4]{0,1:T(4,128)}, f32[256,4]{0,1:T(4,128)S(1)}, f32[256,4,128]{2,0,1:T(8,128)S(1)}) conditional(s32[]{:T(128)} %convert_element_type.174, () %tuple.98, (pred[256,256]{0,1:T(8,128)(4,1)S(1)}, bf16[256,4,128]{0,2,1:T(8,128)(2,1)S(1)}, bf16[256,128]{1,0:T(8,128)(2,1)}, bf16[256,128]{1,0:T(8,128)(2,1)}) %tuple.293), branch_computations={%region_31.32_spmd, %region_32.35_spmd} | conditional | flops 136712192 | bytes 4304920 | solution.py:98
  127.2 1.1 fusion.194
  128.4 0.6 exponential_multiply_fusion
  129.0 1.3 convolution_add_fusion
  130.2 0.9 fusion.2
  131.1 0.7 fusion.10
  131.8 3.0 %conditional.16 = ((f32[256,4]{0,1:T(4,128)}, f32[256,4]{0,1:T(4,128)S(1)}, f32[256,4,128]{2,0,1:T(8,128)S(1)})) conditional(s32[]{:T(128)} %convert_element_type.173, (f32[256,4]{0,1:T(4,128)}, f32[256,4]{0,1:T(4,128)S(1)}, f32[256,4,128]{2,0,1:T(8,128)S(1)}) %conditional.15, (pred[256,256]{0,1:T(8,128)(4,1)S(1)}, ...), branch_computations={%region_35.36_spmd, %region_36.39_spmd} | conditional | flops 136841216 | bytes 4849696 | solution.py:98
  132.1 0.7 max.28
  133.0 0.7 multiply_add_fusion
  134.8 3.0 %conditional.17 = ((f32[256,4]{0,1:T(4,128)}, f32[256,4]{0,1:T(4,128)S(1)}, f32[256,4,128]{2,0,1:T(8,128)S(1)})) conditional(s32[]{:T(128)} %convert_element_type.171, (f32[256,4]{0,1:T(4,128)}, f32[256,4]{0,1:T(4,128)S(1)}, f32[256,4,128]{2,0,1:T(8,128)S(1)}) %get-tuple-element.849, (pred[256,256]{0,1:T(8,128)(4,1)S(1)}, ...), branch_computations={%region_39.40_spmd, %region_40.43_spmd} | conditional | flops 136841216 | bytes 4849696 | solution.py:98
  135.1 0.7 max.29
  136.0 0.7 multiply_add_fusion.1
  137.8 3.0 %conditional.19 = ((f32[256,4]{0,1:T(4,128)}, f32[256,4]{0,1:T(4,128)S(1)}, f32[256,4,128]{2,0,1:T(8,128)S(1)})) conditional(s32[]{:T(128)} %convert_element_type.167, (f32[256,4]{0,1:T(4,128)}, f32[256,4]{0,1:T(4,128)S(1)}, f32[256,4,128]{2,0,1:T(8,128)S(1)}) %get-tuple-element.851, (pred[256,256]{0,1:T(8,128)(4,1)S(1)}, ...), branch_computations={%region_47.48_spmd, %region_48.51_spmd} | conditional | flops 136841216 | bytes 4849696 | solution.py:98
  138.1 0.7 max.31
  139.0 0.7 multiply_add_fusion.3
  140.8 3.0 %conditional.21 = ((f32[256,4]{0,1:T(4,128)}, f32[256,4]{0,1:T(4,128)S(1)}, f32[256,4,128]{2,0,1:T(8,128)S(1)})) conditional(s32[]{:T(128)} %convert_element_type.163, (f32[256,4]{0,1:T(4,128)}, f32[256,4]{0,1:T(4,128)S(1)}, f32[256,4,128]{2,0,1:T(8,128)S(1)}) %get-tuple-element.853, (pred[256,256]{0,1:T(8,128)(4,1)S(1)}, ...), branch_computations={%region_55.56_spmd, %region_56.59_spmd} | conditional | flops 136841216 | bytes 4849696 | solution.py:98
  141.1 0.7 max.33
  142.0 0.7 multiply_add_fusion.5
  143.8 3.0 %conditional.23 = ((f32[256,4]{0,1:T(4,128)}, f32[256,4]{0,1:T(4,128)S(1)}, f32[256,4,128]{2,0,1:T(8,128)S(1)})) conditional(s32[]{:T(128)} %convert_element_type.159, (f32[256,4]{0,1:T(4,128)}, f32[256,4]{0,1:T(4,128)S(1)}, f32[256,4,128]{2,0,1:T(8,128)S(1)}) %get-tuple-element.855, (pred[256,256]{0,1:T(8,128)(4,1)S(1)}, ...), branch_computations={%region_63.64_spmd, %region_64.67_spmd} | conditional | flops 136841216 | bytes 4849696 | solution.py:98
  144.1 0.7 max.35
  145.0 0.7 multiply_add_fusion.7
  146.8 3.0 %conditional.25 = ((f32[256,4]{0,1:T(4,128)}, f32[256,4]{0,1:T(4,128)S(1)}, f32[256,4,128]{2,0,1:T(8,128)S(1)})) conditional(s32[]{:T(128)} %convert_element_type.155, (f32[256,4]{0,1:T(4,128)}, f32[256,4]{0,1:T(4,128)S(1)}, f32[256,4,128]{2,0,1:T(8,128)S(1)}) %get-tuple-element.857, (pred[256,256]{0,1:T(8,128)(4,1)S(1)}, ...), branch_computations={%region_71.72_spmd, %region_72.75_spmd} | conditional | flops 136841216 | bytes 4849696 | solution.py:98
  147.1 0.7 max.37
  148.0 0.7 multiply_add_fusion.9
  149.8 1.3 conditional.27
  149.8 1.3 copy.192
  151.3 4.8 %convolution_convert_fusion = bf16[256,4096]{1,0:T(8,128)(2,1)} fusion(bf16[256,512]{0,1:T(8,128)(2,1)S(1)} %bitcast.185, bf16[512,4096]{1,0:T(8,128)(2,1)} %param.39), kind=kOutput, calls=%fused_computation.239 | convolution fusion | flops 1074790400 | bytes 6553600 | tf_op jit(solution)/shard_map/dot_general | solution.py:105
  156.2 99.2 %reduce-scatter.2.cloned.1.call-done = bf16[32,4096]{1,0:T(8,128)(2,1)} async-done(((bf16[256,4096]{1,0:T(8,128)(2,1)}), bf16[32,4096]{1,0:T(8,128)(2,1)}) %reduce-scatter.2.cloned.1.call-update) | async-done | bytes 262160 | tf_op jit(solution)/shard_map/reduce_scatter | solution.py:104
  (64 shorter events, 10.6 us)
Async XLA Ops:
  6.5 248.8 %reduce-scatter.2.cloned.1.call-start = ((), (), s32[]{:S(2)}) async-start(), calls=%async_computation.1 | async-start | bytes 2359296 | tf_op jit(solution)/shard_map/reduce_scatter | solution.py:104
  8.1 22.1 %collective-permute-start = (bf16[2,256,128]{2,1,0:T(8,128)(2,1)}, bf16[2,256,128]{2,1,0:T(8,128)(2,1)S(1)}, u32[]{:S(2)}, u32[]{:S(2)}) collective-permute-start(bf16[2,256,128]{2,1,0:T(8,128)(2,1)} %pad_maximum_fusion), channel_id=1, source_target_pairs={{0,8},{8,16},{16,24},{24,32},{32,40},{40,48},{48,56},{56,64},{64,7... | collective-permute-start | bytes 393224 | tf_op jit(solution)/shard_map/ppermute | solution.py:18
  10.0 26.2 %collective-permute-start.1 = (bf16[2,256,128]{2,1,0:T(8,128)(2,1)}, bf16[2,256,128]{2,1,0:T(8,128)(2,1)S(1)}, u32[]{:S(2)}, u32[]{:S(2)}) collective-permute-start(bf16[2,256,128]{2,1,0:T(8,128)(2,1)} %pad_maximum_fusion), channel_id=1, source_target_pairs={{8,0},{16,8},{24,16},{32,24},{40,32},{48,40},{56,48},{64,56},{72,6... | collective-permute-start | bytes 393224 | tf_op jit(solution)/shard_map/ppermute | solution.py:18
  15.8 29.3 %collective-permute-start.2 = (bf16[2,256,128]{2,1,0:T(8,128)(2,1)}, bf16[2,256,128]{2,1,0:T(8,128)(2,1)S(1)}, u32[]{:S(2)}, u32[]{:S(2)}) collective-permute-start(bf16[2,256,128]{2,1,0:T(8,128)(2,1)} %pad_maximum_fusion), channel_id=1, source_target_pairs={{0,16},{8,24},{16,32},{24,40},{32,48},{40,56},{48,64},{56,72},{64,... | collective-permute-start | bytes 393224 | tf_op jit(solution)/shard_map/ppermute | solution.py:18
  17.7 29.3 %collective-permute-start.3 = (bf16[2,256,128]{2,1,0:T(8,128)(2,1)}, bf16[2,256,128]{2,1,0:T(8,128)(2,1)S(1)}, u32[]{:S(2)}, u32[]{:S(2)}) collective-permute-start(bf16[2,256,128]{2,1,0:T(8,128)(2,1)} %pad_maximum_fusion), channel_id=1, source_target_pairs={{16,0},{24,8},{32,16},{40,24},{48,32},{56,40},{64,48},{72,56},{80,... | collective-permute-start | bytes 393224 | tf_op jit(solution)/shard_map/ppermute | solution.py:18
  23.7 57.1 %collective-permute-start.4 = (bf16[2,256,128]{2,1,0:T(8,128)(2,1)}, bf16[2,256,128]{2,1,0:T(8,128)(2,1)S(1)}, u32[]{:S(2)}, u32[]{:S(2)}) collective-permute-start(bf16[2,256,128]{2,1,0:T(8,128)(2,1)} %pad_maximum_fusion), channel_id=1, source_target_pairs={{0,24},{8,32},{16,40},{24,48},{32,56},{40,64},{48,72},{56,80},{64,... | collective-permute-start | bytes 393224 | tf_op jit(solution)/shard_map/ppermute | solution.py:18
  30.2 52.6 %collective-permute-start.5 = (bf16[2,256,128]{2,1,0:T(8,128)(2,1)}, bf16[2,256,128]{2,1,0:T(8,128)(2,1)S(1)}, u32[]{:S(2)}, u32[]{:S(2)}) collective-permute-start(bf16[2,256,128]{2,1,0:T(8,128)(2,1)} %pad_maximum_fusion), channel_id=1, source_target_pairs={{24,0},{32,8},{40,16},{48,24},{56,32},{64,40},{72,48},{80,56},{88,... | collective-permute-start | bytes 393224 | tf_op jit(solution)/shard_map/ppermute | solution.py:18
  36.2 61.3 %collective-permute-start.6 = (bf16[2,256,128]{2,1,0:T(8,128)(2,1)}, bf16[2,256,128]{2,1,0:T(8,128)(2,1)S(1)}, u32[]{:S(2)}, u32[]{:S(2)}) collective-permute-start(bf16[2,256,128]{2,1,0:T(8,128)(2,1)} %pad_maximum_fusion), channel_id=1, source_target_pairs={{0,32},{8,40},{16,48},{24,56},{32,64},{40,72},{48,80},{56,88},{64,... | collective-permute-start | bytes 393224 | tf_op jit(solution)/shard_map/ppermute | solution.py:18
  45.1 54.4 %collective-permute-start.7 = (bf16[2,256,128]{2,1,0:T(8,128)(2,1)}, bf16[2,256,128]{2,1,0:T(8,128)(2,1)S(1)}, u32[]{:S(2)}, u32[]{:S(2)}) collective-permute-start(bf16[2,256,128]{2,1,0:T(8,128)(2,1)} %pad_maximum_fusion), channel_id=1, source_target_pairs={{32,0},{40,8},{48,16},{56,24},{64,32},{72,40},{80,48},{88,56},{96,... | collective-permute-start | bytes 393224 | tf_op jit(solution)/shard_map/ppermute | solution.py:18
  47.0 69.0 %collective-permute-start.8 = (bf16[2,256,128]{2,1,0:T(8,128)(2,1)}, bf16[2,256,128]{2,1,0:T(8,128)(2,1)S(1)}, u32[]{:S(2)}, u32[]{:S(2)}) collective-permute-start(bf16[2,256,128]{2,1,0:T(8,128)(2,1)} %pad_maximum_fusion), channel_id=1, source_target_pairs={{0,40},{8,48},{16,56},{24,64},{32,72},{40,80},{48,88},{56,96},{64,... | collective-permute-start | bytes 393224 | tf_op jit(solution)/shard_map/ppermute | solution.py:18
  80.8 66.0 %collective-permute-start.9 = (bf16[2,256,128]{2,1,0:T(8,128)(2,1)}, bf16[2,256,128]{2,1,0:T(8,128)(2,1)S(1)}, u32[]{:S(2)}, u32[]{:S(2)}) collective-permute-start(bf16[2,256,128]{2,1,0:T(8,128)(2,1)} %pad_maximum_fusion), channel_id=1, source_target_pairs={{40,0},{48,8},{56,16},{64,24},{72,32},{80,40},{88,48},{96,56},{104... | collective-permute-start | bytes 393224 | tf_op jit(solution)/shard_map/ppermute | solution.py:18
  82.7 14.8 %copy-start = (bf16[2,256,128]{2,1,0:T(8,128)(2,1)}, bf16[2,256,128]{2,1,0:T(8,128)(2,1)S(1)}, u32[]{:S(2)}) copy-start(bf16[2,256,128]{2,1,0:T(8,128)(2,1)S(1)} %collective-permute-done.5) | copy-start | bytes 393220
  82.8 67.0 %collective-permute-start.10 = (bf16[2,256,128]{2,1,0:T(8,128)(2,1)}, bf16[2,256,128]{2,1,0:T(8,128)(2,1)S(1)}, u32[]{:S(2)}, u32[]{:S(2)}) collective-permute-start(bf16[2,256,128]{2,1,0:T(8,128)(2,1)} %pad_maximum_fusion), channel_id=1, source_target_pairs={{0,48},{8,56},{16,64},{24,72},{32,80},{40,88},{48,96},{56,104},{64... | collective-permute-start | bytes 393224 | tf_op jit(solution)/shard_map/ppermute | solution.py:18
  97.6 52.2 %collective-permute-start.11 = (bf16[2,256,128]{2,1,0:T(8,128)(2,1)}, bf16[2,256,128]{2,1,0:T(8,128)(2,1)S(1)}, u32[]{:S(2)}, u32[]{:S(2)}) collective-permute-start(bf16[2,256,128]{2,1,0:T(8,128)(2,1)} %pad_maximum_fusion), channel_id=1, source_target_pairs={{48,0},{56,8},{64,16},{72,24},{80,32},{88,40},{96,48},{104,56},{11... | collective-permute-start | bytes 393224 | tf_op jit(solution)/shard_map/ppermute | solution.py:18
  99.5 51.5 %collective-permute-start.12 = (bf16[2,256,128]{2,1,0:T(8,128)(2,1)}, bf16[2,256,128]{2,1,0:T(8,128)(2,1)S(1)}, u32[]{:S(2)}, u32[]{:S(2)}) collective-permute-start(bf16[2,256,128]{2,1,0:T(8,128)(2,1)} %pad_maximum_fusion), channel_id=1, source_target_pairs={{0,56},{8,64},{16,72},{24,80},{32,88},{40,96},{48,104},{56,112},{6... | collective-permute-start | bytes 393224 | tf_op jit(solution)/shard_map/ppermute | solution.py:18
  116.1 35.0 %collective-permute-start.13 = (bf16[2,256,128]{2,1,0:T(8,128)(2,1)}, bf16[2,256,128]{2,1,0:T(8,128)(2,1)S(1)}, u32[]{:S(2)}, u32[]{:S(2)}) collective-permute-start(bf16[2,256,128]{2,1,0:T(8,128)(2,1)} %pad_maximum_fusion), channel_id=1, source_target_pairs={{56,0},{64,8},{72,16},{80,24},{88,32},{96,40},{104,48},{112,56},{1... | collective-permute-start | bytes 393224 | tf_op jit(solution)/shard_map/ppermute | solution.py:18
  137.8 3.0 %copy-start.1 = (bf16[2,256,128]{2,1,0:T(8,128)(2,1)S(1)}, bf16[2,256,128]{2,1,0:T(8,128)(2,1)}, u32[]{:S(2)}) copy-start(bf16[2,256,128]{2,1,0:T(8,128)(2,1)} %copy-done) | copy-start | bytes 393220
Sparse Core Ops, SparseCore 0:
  156.3 99.0 reduce-scatter.1
where the time goes:
time: 265 us; the launch traced here: 262 us
  starting transfers between devices  103 us (39%)
  waiting for transfers between devices  99.2 us (37%)
  between operations  23.1 us (9%)
  other arithmetic  17.5 us (7%)
  matrix products  12.1 us (5%)
  local copies, waits for them, and re-layouts  6.83 us (3%)
    ppermute x14, starting transfers between devices, from_behind(): lax.ppermute(value, axis, [(source, source + steps) for source in range(i...  103 us
    reduce_scatter x1, waiting for transfers between devices, local(): lax.psum_scatter(jnp.dot(attention, o_weight, preferred_element_type=jnp....  99.2 us
  transfers between devices with their start and end apart: 15, of which 1 were waited for; matrix products, arithmetic and copies ran while one was open for 11% of the time, Pallas kernels for 0%

commit v1 on v0

v1 whole, which is shorter than its diff:
```python
import math

import jax
import jax.numpy as jnp
from jax import lax
from jax.experimental import pallas as pl
from jax.experimental.pallas import tpu as pltpu
from jax.sharding import PartitionSpec as P

BF = jnp.bfloat16
F32 = jnp.float32
HEAD_WIDTH = 128
STRETCH = 128
GROUP = 8
NEG_FILL = -1e30
SCALE = math.log2(math.e) / math.sqrt(HEAD_WIDTH)
VMEM = pl.BlockSpec(memory_space=pltpu.VMEM)
SMEM = pl.BlockSpec(memory_space=pltpu.SMEM)


def prep_kernel(k_ref, v_ref, low_ref, high_ref, own_ref):
    me = lax.rem(lax.axis_index("ctx"), GROUP)
    low_ref[:STRETCH] = k_ref[:STRETCH]
    low_ref[STRETCH:] = v_ref[:STRETCH]
    high_ref[:STRETCH] = k_ref[STRETCH:]
    high_ref[STRETCH:] = v_ref[STRETCH:]
    for j in range(GROUP):
        @pl.when(j >= me)
        def _():
            own_ref[j] = low_ref[...]

        @pl.when(j < me)
        def _():
            own_ref[j] = high_ref[...]


def pass_kernel(groups, low_ref, high_ref, mirror_ref, out_ref):
    ctx = lax.axis_index("ctx")
    me = lax.rem(ctx, GROUP)
    last = ctx >= (groups - 1) * GROUP
    for j in range(GROUP):
        @pl.when((j >= me) & last)
        def _():
            out_ref[j] = mirror_ref[...]

        @pl.when((j >= me) & jnp.logical_not(last))
        def _():
            out_ref[j] = high_ref[...]

        @pl.when(j < me)
        def _():
            out_ref[j] = low_ref[...]


def main_kernel(stretches, docs, q_ref, k_ref, v_ref, own_ref, sh_ref, len_ref, w_hbm, *rest):
    outs, (kbuf, vbuf, bias, attn, rows, wbuf, sem) = rest[:8], rest[8:]
    ctx = lax.axis_index("ctx")
    kvh = lax.axis_index("kvh")
    me = lax.rem(ctx, GROUP)
    group0 = ctx - me
    copy = pltpu.make_async_copy(w_hbm, wbuf, sem)
    copy.start()
    heads = q_ref.shape[1] // HEAD_WIDTH
    row = lax.broadcasted_iota(jnp.int32, (STRETCH, HEAD_WIDTH), 0)
    lane = lax.broadcasted_iota(jnp.int32, (STRETCH, HEAD_WIDTH), 1)
    for chain in range(2):
        q_base = (ctx if chain == 0 else stretches - 1 - ctx) * STRETCH
        q_place = q_base + row
        begin = jnp.zeros_like(row)
        end = jnp.int32(0)
        for n in range(docs):
            end = end + len_ref[n]
            begin = jnp.where(end <= q_place, end, begin)
        for s in range(GROUP):
            here = pl.ds(s * STRETCH, STRETCH)
            if chain == 0:
                near = s <= me
                source = group0 + s - jnp.where(near, 0, GROUP)
                key_base = source * STRETCH
            else:
                near = s >= me
                source = group0 + s + jnp.where(near, 0, GROUP)
                key_base = (stretches - 1 - source) * STRETCH

            @pl.when(near)
            def _():
                kbuf[here] = own_ref[s, :STRETCH]
                vbuf[here] = own_ref[s, STRETCH:]

            @pl.when(jnp.logical_not(near))
            def _():
                kbuf[here] = sh_ref[s, :STRETCH]
                vbuf[here] = sh_ref[s, STRETCH:]

            if chain == 1:
                @pl.when(s == me)
                def _():
                    kbuf[here] = k_ref[STRETCH:]
                    vbuf[here] = v_ref[STRETCH:]

            key_place = key_base + lane
            allowed = (key_place >= begin) & (key_place <= q_place)
            bias[:, here] = jnp.where(allowed, 0.0, NEG_FILL)
        mine = pl.ds(chain * STRETCH, STRETCH)
        for h in range(heads):
            columns = pl.ds(h * HEAD_WIDTH, HEAD_WIDTH)
            scores = lax.dot_general(
                q_ref[mine, columns], kbuf[...], (((1,), (1,)), ((), ())), preferred_element_type=F32
            )
            scores = scores * SCALE + bias[...]
            highest = jnp.max(scores, axis=1, keepdims=True)
            weights = jnp.exp2(scores - highest)
            total = jnp.sum(weights, axis=1, keepdims=True)
            result = jnp.dot(weights.astype(BF), vbuf[...], preferred_element_type=F32)
            attn[mine, columns] = (result / total).astype(BF)
    n_kvh = len(outs)
    chunk = attn.shape[0] // n_kvh
    position = jnp.where(lax.rem(kvh, 2) == 0, kvh // 2, n_kvh - 1 - kvh // 2)
    for o in range(n_kvh):
        i = lax.rem(position + o, n_kvh)
        to = jnp.where(i < n_kvh // 2, 2 * i, 2 * n_kvh - 1 - 2 * i)
        rows[pl.ds(o * chunk, chunk)] = attn[pl.ds(pl.multiple_of(to * chunk, chunk), chunk)]
    copy.wait()
    width = 512
    for c in range(wbuf.shape[1] // width):
        columns = pl.ds(c * width, width)
        part = jnp.dot(rows[...], wbuf[:, columns], preferred_element_type=F32).astype(BF)
        for o in range(n_kvh):
            outs[o][:, columns] = part[o * chunk : (o + 1) * chunk]


def local(doc_lengths, queries, keys, values, o_weight):
    n_ctx = lax.axis_size("ctx")
    n_kvh = lax.axis_size("kvh")
    groups = n_ctx // GROUP
    pair = jax.ShapeDtypeStruct((2 * STRETCH, HEAD_WIDTH), BF)
    eight = jax.ShapeDtypeStruct((GROUP, 2 * STRETCH, HEAD_WIDTH), BF)
    low, high, own = pl.pallas_call(
        prep_kernel, out_shape=(pair, pair, eight), in_specs=[VMEM] * 2, out_specs=(VMEM,) * 3, name="prep"
    )(keys, values)
    top = n_ctx - GROUP
    mirror = lax.ppermute(low, "ctx", [(top + m, n_ctx - 1 - m) for m in range(GROUP)])
    low_in = lax.ppermute(low, "ctx", [(i, i + GROUP) for i in range(n_ctx - GROUP)])
    high_in = lax.ppermute(high, "ctx", [(i, i - GROUP) for i in range(GROUP, n_ctx)])
    members = [list(range(g * GROUP, (g + 1) * GROUP)) for g in range(groups)]

    def exchange(x):
        return lax.all_to_all(x, "ctx", 0, 0, axis_index_groups=members, tiled=True)

    own = exchange(own)
    passed = pl.pallas_call(
        lambda *refs: pass_kernel(groups, *refs),
        out_shape=eight,
        in_specs=[VMEM] * 3,
        out_specs=VMEM,
        name="pass",
    )(low_in, high_in, mirror)
    passed = exchange(passed)
    rows, inner = queries.shape
    width = o_weight.shape[1]
    keys_all = GROUP * STRETCH
    chunk = jax.ShapeDtypeStruct((rows // n_kvh, width), BF)
    part = pl.pallas_call(
        lambda *refs: main_kernel(2 * n_ctx, doc_lengths.shape[0], *refs),
        out_shape=(chunk,) * n_kvh,
        in_specs=[VMEM] * 5 + [SMEM, pl.BlockSpec(memory_space=pl.ANY)],
        out_specs=(VMEM,) * n_kvh,
        scratch_shapes=[
            pltpu.VMEM((keys_all, HEAD_WIDTH), BF),
            pltpu.VMEM((keys_all, HEAD_WIDTH), BF),
            pltpu.VMEM((STRETCH, keys_all), F32),
            pltpu.VMEM((rows, inner), BF),
            pltpu.VMEM((rows, inner), BF),
            pltpu.VMEM(o_weight.shape, BF),
            pltpu.SemaphoreType.DMA,
        ],
        name="attend",
    )(queries, keys, values, own, passed, doc_lengths, o_weight)

    ring = list(range(0, n_kvh, 2)) + list(range(n_kvh - 1, 0, -2))
    onward = [(ring[i], ring[(i + 1) % n_kvh]) for i in range(n_kvh)]
    back = [(to, source) for source, to in onward]

    def add(a, b):
        return (a.astype(F32) + b.astype(F32)).astype(BF)

    a, b = part[n_kvh // 2], part[n_kvh // 2 + 1]
    for distance in range(n_kvh // 2, 1, -1):
        a = add(part[distance - 1], lax.ppermute(a, "kvh", onward))
        b = lax.ppermute(b, "kvh", back)
        if distance > 2:
            b = add(part[n_kvh + 2 - distance], b)
            a, b = lax.optimization_barrier((a, b))
    a = lax.ppermute(a, "kvh", onward)
    return (part[0].astype(F32) + a.astype(F32) + b.astype(F32)).astype(BF)


def solution(mesh):
    in_specs = (P(), P("ctx", "kvh"), P("ctx", "kvh"), P("ctx", "kvh"), P("kvh", None))
    out_specs = P(("ctx", "kvh"), None)
    return jax.shard_map(local, mesh=mesh, in_specs=in_specs, out_specs=out_specs, check_vma=False)
```

time: 265 us -> 125 us (0.47)
  the two profiles are of different devices: /device:TPU:6 before, /device:TPU:384 now
where the time goes in v1:
time: 125 us; the launch traced here: 124 us
  waiting for transfers between devices  51.9 us (42%)
  starting transfers between devices  38.6 us (31%)
  blocking collectives  14.9 us (12%)
  Pallas kernels  11.1 us (9%)
  other arithmetic  6.82 us (5%)
    ppermute x3, waiting for transfers between devices, local(): a = add(part[distance - 1], lax.ppermute(a, 'kvh', onward))  25.5 us
    ppermute x1, waiting for transfers between devices, local(): lax.ppermute(low, 'ctx', [(i, i + GROUP) for i in range(n_ctx - GROUP)])  15.6 us
    all_to_all x1, blocking collectives, exchange(): return lax.all_to_all(x, 'ctx', 0, 0, axis_index_groups=members, tiled=True)  14.9 us
    ppermute x3, starting transfers between devices, local(): a = add(part[distance - 1], lax.ppermute(a, 'kvh', onward))  13.3 us
    ppermute x3, starting transfers between devices, local(): b = lax.ppermute(b, 'kvh', back)  10.5 us
    ppermute x1, waiting for transfers between devices, local(): a = lax.ppermute(a, 'kvh', onward)  9.19 us
    pallas_call x1, Pallas kernels, local(): pl.pallas_call(lambda *refs: main_kernel(2 * n_ctx, doc_lengths.shape[0],...  7.52 us
    ppermute x1, starting transfers between devices, local(): lax.ppermute(high, 'ctx', [(i, i - GROUP) for i in range(GROUP, n_ctx)])  5.82 us
  transfers between devices with their start and end apart: 11, of which 6 were waited for; matrix products, arithmetic and copies ran while one was open for 2% of the time, Pallas kernels for 1%

profile of v1, /device:TPU:384, one launch (start us, length us, event | category | flops | bytes accessed | tf_op | source)
XLA Modules:
  0.0 124.2 jit_solution(4024941930100654540)
XLA Ops:
  0.0 1.8 %prep.1 = (bf16[256,128]{1,0:T(8,128)(2,1)}, bf16[256,128]{1,0:T(8,128)(2,1)}, bf16[8,256,128]{2,1,0:T(8,128)(2,1)}) custom-call(bf16[256,128]{1,0:T(8,128)(2,1)} %refs_1_.1, bf16[256,128]{1,0:T(8,128)(2,1)} %refs_2_.1), custom_call_target="tpu_custom_call" | custom-call | tf_op jit(solution)/shard_map/prep/pallas_call | solution.py:138
  1.8 4.5 %all-to-all-start = ((bf16[8,256,128]{2,1,0:T(8,128)(2,1)}), bf16[8,256,128]{2,1,0:T(8,128)(2,1)S(1)}, u32[]{:S(2)}, u32[]{:S(2)}) async-start(bf16[8,256,128]{2,1,0:T(8,128)(2,1)} %get-tuple-element.20), calls=%async_computation | async-start | bytes 1048576 | tf_op jit(solution)/shard_map/all_to_all | solution.py:148
  6.2 5.8 %collective-permute-start.1 = (bf16[256,128]{1,0:T(8,128)(2,1)}, bf16[256,128]{1,0:T(8,128)(2,1)S(1)}, u32[]{:S(2)}, u32[]{:S(2)}) collective-permute-start(bf16[256,128]{1,0:T(8,128)(2,1)} %get-tuple-element.22), channel_id=1, source_target_pairs={{64,0},{72,8},{80,16},{88,24},{96,32},{104,40},{112,48},{120,56},{... | collective-permute-start | bytes 196616 | tf_op jit(solution)/shard_map/ppermute | solution.py:144
  12.1 0.7 collective-permute-start.2
  12.7 1.9 %collective-permute-start = (bf16[256,128]{1,0:T(8,128)(2,1)}, bf16[256,128]{1,0:T(8,128)(2,1)S(1)}, u32[]{:S(2)}, u32[]{:S(2)}) collective-permute-start(bf16[256,128]{1,0:T(8,128)(2,1)} %get-tuple-element.21), channel_id=1, source_target_pairs={{0,64},{8,72},{16,80},{24,88},{32,96},{40,104},{48,112},{56,120},{... | collective-permute-start | bytes 196616 | tf_op jit(solution)/shard_map/ppermute | solution.py:143
  14.7 1.6 %collective-permute-done.1.refs_1_ = bf16[256,128]{1,0:T(8,128)(2,1)S(1)} collective-permute-done((bf16[256,128]{1,0:T(8,128)(2,1)}, bf16[256,128]{1,0:T(8,128)(2,1)S(1)}, u32[]{:S(2)}, u32[]{:S(2)}) %collective-permute-start.1) | collective-permute-done | bytes 65568 | tf_op jit(solution)/shard_map/ppermute | solution.py:144
  16.3 0.0 copy-start.1
  16.3 0.0 collective-permute-done.2.refs_2_
  16.3 0.0 copy-start.2
  16.3 15.6 %collective-permute-done.refs_0_ = bf16[256,128]{1,0:T(8,128)(2,1)S(1)} collective-permute-done((bf16[256,128]{1,0:T(8,128)(2,1)}, bf16[256,128]{1,0:T(8,128)(2,1)S(1)}, u32[]{:S(2)}, u32[]{:S(2)}) %collective-permute-start) | collective-permute-done | bytes 65568 | tf_op jit(solution)/shard_map/ppermute | solution.py:143
  31.9 0.0 copy-done.1
  31.9 0.0 copy-done.2
  31.9 0.0 copy-start.3
  31.9 0.6 copy-done.3
  32.5 1.8 %pass.1 = bf16[8,256,128]{2,1,0:T(8,128)(2,1)} custom-call(bf16[256,128]{1,0:T(8,128)(2,1)} %copy-done.3, bf16[256,128]{1,0:T(8,128)(2,1)} %copy-done.1, bf16[256,128]{1,0:T(8,128)(2,1)} %copy-done.2), custom_call_target="tpu_custom_call" | custom-call | tf_op jit(solution)/shard_map/pass/pallas_call | solution.py:151
  34.3 0.0 all-to-all-done.refs_3_
  34.3 0.0 copy-start
  34.3 14.9 %all_to_all.10.refs_4_ = bf16[8,256,128]{2,1,0:T(8,128)(2,1)} all-to-all(bf16[8,256,128]{2,1,0:T(8,128)(2,1)} %pass.1), channel_id=1, replica_groups={{0,8,16,24,32,40,48,56},{64,72,80,88,96,104,112,120},{128,136,144,152,1..., dimensions={0} | all-to-all | bytes 1048576 | tf_op jit(solution)/shard_map/all_to_all | solution.py:148
  49.2 0.0 copy-done
  49.2 7.5 %attend.1 = (bf16[32,4096]{1,0:T(8,128)(2,1)}, bf16[32,4096]{1,0:T(8,128)(2,1)}, bf16[32,4096]{1,0:T(8,128)(2,1)}, bf16[32,4096]{1,0:T(8,128)(2,1)}, bf16[32,409...) custom-call(bf16[256,512]{1,0:T(8,128)(2,1)} %refs_0_.1, ...), custom_call_target="tpu_custom_call" | custom-call | tf_op jit(solution)/shard_map/attend/pallas_call | solution.py:163
  56.7 5.6 %collective-permute-start.3 = (bf16[32,4096]{1,0:T(8,128)(2,1)}, bf16[32,4096]{1,0:T(8,128)(2,1)S(1)}, u32[]{:S(2)}, u32[]{:S(2)}) collective-permute-start(bf16[32,4096]{1,0:T(8,128)(2,1)} %get-tuple-element.27), channel_id=1, source_target_pairs={{0,2},{2,4},{4,6},{6,7},{7,5},{5,3},{3,1},{1,0},{8,10},{10,12},{12... | collective-permute-start | bytes 786440 | tf_op jit(solution)/shard_map/ppermute | solution.py:189
  62.3 2.4 %collective-permute-start.4 = (bf16[32,4096]{1,0:T(8,128)(2,1)}, bf16[32,4096]{1,0:T(8,128)(2,1)S(1)}, u32[]{:S(2)}, u32[]{:S(2)}) collective-permute-start(bf16[32,4096]{1,0:T(8,128)(2,1)} %get-tuple-element.29), channel_id=1, source_target_pairs={{2,0},{4,2},{6,4},{7,6},{5,7},{3,5},{1,3},{0,1},{10,8},{12,10},{14... | collective-permute-start | bytes 786440 | tf_op jit(solution)/shard_map/ppermute | solution.py:190
  64.7 9.5 %collective-permute-done.3 = bf16[32,4096]{1,0:T(8,128)(2,1)S(1)} collective-permute-done((bf16[32,4096]{1,0:T(8,128)(2,1)}, bf16[32,4096]{1,0:T(8,128)(2,1)S(1)}, u32[]{:S(2)}, u32[]{:S(2)}) %collective-permute-start.3) | collective-permute-done | bytes 262176 | tf_op jit(solution)/shard_map/ppermute | solution.py:189
  74.3 1.0 add_convert_fusion.5
  75.3 0.0 collective-permute-done.4
  75.3 1.0 add_convert_fusion.4
  76.3 4.4 %collective-permute-start.5 = (bf16[32,4096]{1,0:T(8,128)(2,1)S(1)}, bf16[32,4096]{1,0:T(8,128)(2,1)S(1)}, u32[]{:S(2)}, u32[]{:S(2)}) collective-permute-start(bf16[32,4096]{1,0:T(8,128)(2,1)S(1)} %add_convert_fusion.5), channel_id=1, source_target_pairs={{0,2},{2,4},{4,6},{6,7},{7,5},{5,3},{3,1},{1,0},{8,10},{10,12},{12... | collective-permute-start | bytes 786440 | tf_op jit(solution)/shard_map/ppermute | solution.py:189
  80.7 3.6 %collective-permute-start.6 = (bf16[32,4096]{1,0:T(8,128)(2,1)S(1)}, bf16[32,4096]{1,0:T(8,128)(2,1)S(1)}, u32[]{:S(2)}, u32[]{:S(2)}) collective-permute-start(bf16[32,4096]{1,0:T(8,128)(2,1)S(1)} %add_convert_fusion.4), channel_id=1, source_target_pairs={{2,0},{4,2},{6,4},{7,6},{5,7},{3,5},{1,3},{0,1},{10,8},{12,10},{14... | collective-permute-start | bytes 786440 | tf_op jit(solution)/shard_map/ppermute | solution.py:190
  84.3 8.4 %collective-permute-done.5 = bf16[32,4096]{1,0:T(8,128)(2,1)S(1)} collective-permute-done((bf16[32,4096]{1,0:T(8,128)(2,1)S(1)}, bf16[32,4096]{1,0:T(8,128)(2,1)S(1)}, u32[]{:S(2)}, u32[]{:S(2)}) %collective-permute-start.5) | collective-permute-done | bytes 262176 | tf_op jit(solution)/shard_map/ppermute | solution.py:189
  92.7 1.0 add_convert_fusion.3
  93.7 0.0 collective-permute-done.6
  93.7 1.0 add_convert_fusion.2
  94.7 3.4 %collective-permute-start.7 = (bf16[32,4096]{1,0:T(8,128)(2,1)S(1)}, bf16[32,4096]{1,0:T(8,128)(2,1)S(1)}, u32[]{:S(2)}, u32[]{:S(2)}) collective-permute-start(bf16[32,4096]{1,0:T(8,128)(2,1)S(1)} %add_convert_fusion.3), channel_id=1, source_target_pairs={{0,2},{2,4},{4,6},{6,7},{7,5},{5,3},{3,1},{1,0},{8,10},{10,12},{12... | collective-permute-start | bytes 786440 | tf_op jit(solution)/shard_map/ppermute | solution.py:189
  98.1 4.6 %collective-permute-start.9 = (bf16[32,4096]{1,0:T(8,128)(2,1)S(1)}, bf16[32,4096]{1,0:T(8,128)(2,1)S(1)}, u32[]{:S(2)}, u32[]{:S(2)}) collective-permute-start(bf16[32,4096]{1,0:T(8,128)(2,1)S(1)} %add_convert_fusion.2), channel_id=1, source_target_pairs={{2,0},{4,2},{6,4},{7,6},{5,7},{3,5},{1,3},{0,1},{10,8},{12,10},{14... | collective-permute-start | bytes 786440 | tf_op jit(solution)/shard_map/ppermute | solution.py:190
  102.7 7.6 %collective-permute-done.7 = bf16[32,4096]{1,0:T(8,128)(2,1)S(1)} collective-permute-done((bf16[32,4096]{1,0:T(8,128)(2,1)S(1)}, bf16[32,4096]{1,0:T(8,128)(2,1)S(1)}, u32[]{:S(2)}, u32[]{:S(2)}) %collective-permute-start.7) | collective-permute-done | bytes 262176 | tf_op jit(solution)/shard_map/ppermute | solution.py:189
  110.3 1.0 add_convert_fusion.1
  111.3 1.9 %collective-permute-start.8 = (bf16[32,4096]{1,0:T(8,128)(2,1)S(1)}, bf16[32,4096]{1,0:T(8,128)(2,1)S(1)}, u32[]{:S(2)}, u32[]{:S(2)}) collective-permute-start(bf16[32,4096]{1,0:T(8,128)(2,1)S(1)} %add_convert_fusion.1), channel_id=1, source_target_pairs={{0,2},{2,4},{4,6},{6,7},{7,5},{5,3},{3,1},{1,0},{8,10},{10,12},{12... | collective-permute-start | bytes 786440 | tf_op jit(solution)/shard_map/ppermute | solution.py:194
  113.2 0.0 collective-permute-done.9
  113.2 9.2 %collective-permute-done.8 = bf16[32,4096]{1,0:T(8,128)(2,1)S(1)} collective-permute-done((bf16[32,4096]{1,0:T(8,128)(2,1)S(1)}, bf16[32,4096]{1,0:T(8,128)(2,1)S(1)}, u32[]{:S(2)}, u32[]{:S(2)}) %collective-permute-start.8) | collective-permute-done | bytes 262176 | tf_op jit(solution)/shard_map/ppermute | solution.py:194
  122.4 1.7 %add_convert_fusion = bf16[32,4096]{1,0:T(8,128)(2,1)} fusion(bf16[32,4096]{1,0:T(8,128)(2,1)S(1)} %collective-permute-done.9, bf16[32,4096]{1,0:T(8,128)(2,1)S(1)} %collective-permute-done.8, bf16[32,4096]{1,0:T(8,128)(2,1)} %get-tuple-element.23), kind=kLoop, calls=%fused_computation | loop fusion | flops 786432 | bytes 1048576 | tf_op jit(solution)/shard_map/convert_element_type | solution.py:195
Async XLA Ops:
  1.8 32.6 %all-to-all-start = ((bf16[8,256,128]{2,1,0:T(8,128)(2,1)}), bf16[8,256,128]{2,1,0:T(8,128)(2,1)S(1)}, u32[]{:S(2)}, u32[]{:S(2)}) async-start(bf16[8,256,128]{2,1,0:T(8,128)(2,1)} %get-tuple-element.20), calls=%async_computation | async-start | bytes 1048576 | tf_op jit(solution)/shard_map/all_to_all | solution.py:148
  6.2 10.0 %collective-permute-start.1 = (bf16[256,128]{1,0:T(8,128)(2,1)}, bf16[256,128]{1,0:T(8,128)(2,1)S(1)}, u32[]{:S(2)}, u32[]{:S(2)}) collective-permute-start(bf16[256,128]{1,0:T(8,128)(2,1)} %get-tuple-element.22), channel_id=1, source_target_pairs={{64,0},{72,8},{80,16},{88,24},{96,32},{104,40},{112,48},{120,56},{... | collective-permute-start | bytes 196616 | tf_op jit(solution)/shard_map/ppermute | solution.py:144
  12.1 4.2 %collective-permute-start.2 = (bf16[256,128]{1,0:T(8,128)(2,1)}, bf16[256,128]{1,0:T(8,128)(2,1)S(1)}, u32[]{:S(2)}, u32[]{:S(2)}) collective-permute-start(bf16[256,128]{1,0:T(8,128)(2,1)} %get-tuple-element.21), channel_id=1, source_target_pairs={{448,504},{456,496},{464,488},{472,480},{480,472},{488,464},{496,4... | collective-permute-start | bytes 196616 | tf_op jit(solution)/shard_map/ppermute | solution.py:142
  12.7 19.1 %collective-permute-start = (bf16[256,128]{1,0:T(8,128)(2,1)}, bf16[256,128]{1,0:T(8,128)(2,1)S(1)}, u32[]{:S(2)}, u32[]{:S(2)}) collective-permute-start(bf16[256,128]{1,0:T(8,128)(2,1)} %get-tuple-element.21), channel_id=1, source_target_pairs={{0,64},{8,72},{16,80},{24,88},{32,96},{40,104},{48,112},{56,120},{... | collective-permute-start | bytes 196616 | tf_op jit(solution)/shard_map/ppermute | solution.py:143
  16.3 15.6 %copy-start.1 = (bf16[256,128]{1,0:T(8,128)(2,1)}, bf16[256,128]{1,0:T(8,128)(2,1)S(1)}, u32[]{:S(2)}) copy-start(bf16[256,128]{1,0:T(8,128)(2,1)S(1)} %collective-permute-done.1.refs_1_) | copy-start | bytes 196612
  16.3 15.6 %copy-start.2 = (bf16[256,128]{1,0:T(8,128)(2,1)}, bf16[256,128]{1,0:T(8,128)(2,1)S(1)}, u32[]{:S(2)}) copy-start(bf16[256,128]{1,0:T(8,128)(2,1)S(1)} %collective-permute-done.2.refs_2_) | copy-start | bytes 196612
  31.9 0.6 copy-start.3
  34.3 14.9 %copy-start = (bf16[8,256,128]{2,1,0:T(8,128)(2,1)}, bf16[8,256,128]{2,1,0:T(8,128)(2,1)S(1)}, u32[]{:S(2)}) copy-start(bf16[8,256,128]{2,1,0:T(8,128)(2,1)S(1)} %all-to-all-done.refs_3_) | copy-start | bytes 1572868
  56.7 17.5 %collective-permute-start.3 = (bf16[32,4096]{1,0:T(8,128)(2,1)}, bf16[32,4096]{1,0:T(8,128)(2,1)S(1)}, u32[]{:S(2)}, u32[]{:S(2)}) collective-permute-start(bf16[32,4096]{1,0:T(8,128)(2,1)} %get-tuple-element.27), channel_id=1, source_target_pairs={{0,2},{2,4},{4,6},{6,7},{7,5},{5,3},{3,1},{1,0},{8,10},{10,12},{12... | collective-permute-start | bytes 786440 | tf_op jit(solution)/shard_map/ppermute | solution.py:189
  62.3 13.0 %collective-permute-start.4 = (bf16[32,4096]{1,0:T(8,128)(2,1)}, bf16[32,4096]{1,0:T(8,128)(2,1)S(1)}, u32[]{:S(2)}, u32[]{:S(2)}) collective-permute-start(bf16[32,4096]{1,0:T(8,128)(2,1)} %get-tuple-element.29), channel_id=1, source_target_pairs={{2,0},{4,2},{6,4},{7,6},{5,7},{3,5},{1,3},{0,1},{10,8},{12,10},{14... | collective-permute-start | bytes 786440 | tf_op jit(solution)/shard_map/ppermute | solution.py:190
  76.3 16.3 %collective-permute-start.5 = (bf16[32,4096]{1,0:T(8,128)(2,1)S(1)}, bf16[32,4096]{1,0:T(8,128)(2,1)S(1)}, u32[]{:S(2)}, u32[]{:S(2)}) collective-permute-start(bf16[32,4096]{1,0:T(8,128)(2,1)S(1)} %add_convert_fusion.5), channel_id=1, source_target_pairs={{0,2},{2,4},{4,6},{6,7},{7,5},{5,3},{3,1},{1,0},{8,10},{10,12},{12... | collective-permute-start | bytes 786440 | tf_op jit(solution)/shard_map/ppermute | solution.py:189
  80.7 13.0 %collective-permute-start.6 = (bf16[32,4096]{1,0:T(8,128)(2,1)S(1)}, bf16[32,4096]{1,0:T(8,128)(2,1)S(1)}, u32[]{:S(2)}, u32[]{:S(2)}) collective-permute-start(bf16[32,4096]{1,0:T(8,128)(2,1)S(1)} %add_convert_fusion.4), channel_id=1, source_target_pairs={{2,0},{4,2},{6,4},{7,6},{5,7},{3,5},{1,3},{0,1},{10,8},{12,10},{14... | collective-permute-start | bytes 786440 | tf_op jit(solution)/shard_map/ppermute | solution.py:190
  94.7 15.6 %collective-permute-start.7 = (bf16[32,4096]{1,0:T(8,128)(2,1)S(1)}, bf16[32,4096]{1,0:T(8,128)(2,1)S(1)}, u32[]{:S(2)}, u32[]{:S(2)}) collective-permute-start(bf16[32,4096]{1,0:T(8,128)(2,1)S(1)} %add_convert_fusion.3), channel_id=1, source_target_pairs={{0,2},{2,4},{4,6},{6,7},{7,5},{5,3},{3,1},{1,0},{8,10},{10,12},{12... | collective-permute-start | bytes 786440 | tf_op jit(solution)/shard_map/ppermute | solution.py:189
  98.1 15.1 %collective-permute-start.9 = (bf16[32,4096]{1,0:T(8,128)(2,1)S(1)}, bf16[32,4096]{1,0:T(8,128)(2,1)S(1)}, u32[]{:S(2)}, u32[]{:S(2)}) collective-permute-start(bf16[32,4096]{1,0:T(8,128)(2,1)S(1)} %add_convert_fusion.2), channel_id=1, source_target_pairs={{2,0},{4,2},{6,4},{7,6},{5,7},{3,5},{1,3},{0,1},{10,8},{12,10},{14... | collective-permute-start | bytes 786440 | tf_op jit(solution)/shard_map/ppermute | solution.py:190
  111.3 11.1 %collective-permute-start.8 = (bf16[32,4096]{1,0:T(8,128)(2,1)S(1)}, bf16[32,4096]{1,0:T(8,128)(2,1)S(1)}, u32[]{:S(2)}, u32[]{:S(2)}) collective-permute-start(bf16[32,4096]{1,0:T(8,128)(2,1)S(1)} %add_convert_fusion.1), channel_id=1, source_target_pairs={{0,2},{2,4},{4,6},{6,7},{7,5},{5,3},{3,1},{1,0},{8,10},{10,12},{12... | collective-permute-start | bytes 786440 | tf_op jit(solution)/shard_map/ppermute | solution.py:194

commit v2 on v1

--- a/solution.py
+++ b/solution.py
@@ -6,6 +6,7 @@
 from jax.experimental import pallas as pl
 from jax.experimental.pallas import tpu as pltpu
 from jax.sharding import PartitionSpec as P
+
 
 BF = jnp.bfloat16
 F32 = jnp.float32
@@ -18,38 +19,50 @@
 SMEM = pl.BlockSpec(memory_space=pltpu.SMEM)
 
 
-def prep_kernel(k_ref, v_ref, low_ref, high_ref, own_ref):
-    me = lax.rem(lax.axis_index("ctx"), GROUP)
-    low_ref[:STRETCH] = k_ref[:STRETCH]
-    low_ref[STRETCH:] = v_ref[:STRETCH]
-    high_ref[:STRETCH] = k_ref[STRETCH:]
-    high_ref[STRETCH:] = v_ref[STRETCH:]
-    for j in range(GROUP):
-        @pl.when(j >= me)
-        def _():
-            own_ref[j] = low_ref[...]
-
-        @pl.when(j < me)
-        def _():
-            own_ref[j] = high_ref[...]
-
-
-def pass_kernel(groups, low_ref, high_ref, mirror_ref, out_ref):
+def prep_kernel(k_ref, v_ref, even_ref, odd_ref, own_ref):
     ctx = lax.axis_index("ctx")
     me = lax.rem(ctx, GROUP)
-    last = ctx >= (groups - 1) * GROUP
+    is_odd = lax.rem(ctx // GROUP, 2) == 1
+
+    def put(ref, at):
+        ref[:STRETCH] = k_ref[at : at + STRETCH]
+        ref[STRETCH:] = v_ref[at : at + STRETCH]
+
+    @pl.when(is_odd)
+    def _():
+        put(odd_ref, 0)
+        put(even_ref, STRETCH)
+
+    @pl.when(jnp.logical_not(is_odd))
+    def _():
+        put(odd_ref, STRETCH)
+        put(even_ref, 0)
+
     for j in range(GROUP):
-        @pl.when((j >= me) & last)
-        def _():
-            out_ref[j] = mirror_ref[...]
-
-        @pl.when((j >= me) & jnp.logical_not(last))
-        def _():
-            out_ref[j] = high_ref[...]
+
+        @pl.when(j >= me)
+        def _():
+            put(own_ref.at[j], 0)
 
         @pl.when(j < me)
         def _():
-            out_ref[j] = low_ref[...]
+            put(own_ref.at[j], STRETCH)
+
+
+def pass_kernel(even_ref, odd_ref, out_ref):
+    ctx = lax.axis_index("ctx")
+    me = lax.rem(ctx, GROUP)
+    is_odd = lax.rem(ctx // GROUP, 2) == 1
+    for j in range(GROUP):
+        from_odd = (j >= me) == is_odd
+
+        @pl.when(from_odd)
+        def _():
+            out_ref[j] = odd_ref[...]
+
+        @pl.when(jnp.logical_not(from_odd))
+        def _():
+            out_ref[j] = even_ref[...]
 
 
 def main_kernel(stretches, docs, q_ref, k_ref, v_ref, own_ref, sh_ref, len_ref, w_hbm, *rest):
@@ -129,37 +142,45 @@
             outs[o][:, columns] = part[o * chunk : (o + 1) * chunk]
 
 
+def near(x):
+    return pltpu.with_memory_space_constraint(x, pltpu.VMEM)
+
+
 def local(doc_lengths, queries, keys, values, o_weight):
     n_ctx = lax.axis_size("ctx")
     n_kvh = lax.axis_size("kvh")
     groups = n_ctx // GROUP
-    pair = jax.ShapeDtypeStruct((2 * STRETCH, HEAD_WIDTH), BF)
-    eight = jax.ShapeDtypeStruct((GROUP, 2 * STRETCH, HEAD_WIDTH), BF)
-    low, high, own = pl.pallas_call(
+    pair = pltpu.VMEM((2 * STRETCH, HEAD_WIDTH), BF)
+    eight = pltpu.VMEM((GROUP, 2 * STRETCH, HEAD_WIDTH), BF)
+    to_even, to_odd, own = pl.pallas_call(
         prep_kernel, out_shape=(pair, pair, eight), in_specs=[VMEM] * 2, out_specs=(VMEM,) * 3, name="prep"
     )(keys, values)
-    top = n_ctx - GROUP
-    mirror = lax.ppermute(low, "ctx", [(top + m, n_ctx - 1 - m) for m in range(GROUP)])
-    low_in = lax.ppermute(low, "ctx", [(i, i + GROUP) for i in range(n_ctx - GROUP)])
-    high_in = lax.ppermute(high, "ctx", [(i, i - GROUP) for i in range(GROUP, n_ctx)])
+
+    def partner(i, odd):
+        up = (i // GROUP) % 2 == odd
+        if up and i >= n_ctx - GROUP:
+            return 2 * n_ctx - GROUP - 1 - i
+        return i + GROUP if up else i - GROUP
+
+    def swap(x, odd):
+        return lax.ppermute(x, "ctx", [(i, partner(i, odd)) for i in range(n_ctx) if partner(i, odd) >= 0])
+
+    odd_in = swap(to_odd, 1)
+    even_in = swap(to_even, 0)
     members = [list(range(g * GROUP, (g + 1) * GROUP)) for g in range(groups)]
 
     def exchange(x):
         return lax.all_to_all(x, "ctx", 0, 0, axis_index_groups=members, tiled=True)
 
     own = exchange(own)
-    passed = pl.pallas_call(
-        lambda *refs: pass_kernel(groups, *refs),
-        out_shape=eight,
-        in_specs=[VMEM] * 3,
-        out_specs=VMEM,
-        name="pass",
-    )(low_in, high_in, mirror)
+    passed = pl.pallas_call(pass_kernel, out_shape=eight, in_specs=[VMEM] * 2, out_specs=VMEM, name="pass")(
+        near(even_in), near(odd_in)
+    )
     passed = exchange(passed)
     rows, inner = queries.shape
     width = o_weight.shape[1]
     keys_all = GROUP * STRETCH
-    chunk = jax.ShapeDtypeStruct((rows // n_kvh, width), BF)
+    chunk = pltpu.VMEM((rows // n_kvh, width), BF)
     part = pl.pallas_call(
         lambda *refs: main_kernel(2 * n_ctx, doc_lengths.shape[0], *refs),
         out_shape=(chunk,) * n_kvh,
@@ -175,7 +196,7 @@
             pltpu.SemaphoreType.DMA,
         ],
         name="attend",
-    )(queries, keys, values, own, passed, doc_lengths, o_weight)
+    )(queries, keys, values, own, near(passed), doc_lengths, o_weight)
 
     ring = list(range(0, n_kvh, 2)) + list(range(n_kvh - 1, 0, -2))
     onward = [(ring[i], ring[(i + 1) % n_kvh]) for i in range(n_kvh)]
@@ -184,14 +205,15 @@
     def add(a, b):
         return (a.astype(F32) + b.astype(F32)).astype(BF)
 
-    a, b = part[n_kvh // 2], part[n_kvh // 2 + 1]
-    for distance in range(n_kvh // 2, 1, -1):
-        a = add(part[distance - 1], lax.ppermute(a, "kvh", onward))
-        b = lax.ppermute(b, "kvh", back)
-        if distance > 2:
-            b = add(part[n_kvh + 2 - distance], b)
-            a, b = lax.optimization_barrier((a, b))
-    a = lax.ppermute(a, "kvh", onward)
+    far = n_kvh // 2
+    a, b = part[far], part[far + 1]
+    for step in range(far):
+        a = lax.ppermute(a, "kvh", onward)
+        if step < far - 1:
+            b = lax.ppermute(b, "kvh", back)
+            a = add(part[far - 1 - step], a)
+            if step < far - 2:
+                b = add(part[far + 2 + step], b)
     return (part[0].astype(F32) + a.astype(F32) + b.astype(F32)).astype(BF)
 
 

time: 125 us -> 111 us (0.89)
  the two profiles are of different devices: /device:TPU:384 before, /device:TPU:352 now
where the time goes in v2:
time: 111 us
  waiting for transfers between devices  50.1 us (45%)
  starting transfers between devices  36.8 us (33%)
  blocking collectives  14.7 us (13%)
  Pallas kernels  7.91 us (7%)
  other arithmetic  1.12 us (1%)
    ppermute x4, waiting for transfers between devices, local(): a = lax.ppermute(a, 'kvh', onward)  31.8 us
    ppermute x2, waiting for transfers between devices, swap(): lax.ppermute(x, 'ctx', [(i, partner(i, odd)) for i in range(n_ctx) if par...  16.8 us
    all_to_all x1, blocking collectives, exchange(): return lax.all_to_all(x, 'ctx', 0, 0, axis_index_groups=members, tiled=True)  14.7 us
    ppermute x3, starting transfers between devices, local(): b = lax.ppermute(b, 'kvh', back)  13.7 us
    ppermute x4, starting transfers between devices, local(): a = lax.ppermute(a, 'kvh', onward)  12.2 us
    ppermute x2, starting transfers between devices, swap(): lax.ppermute(x, 'ctx', [(i, partner(i, odd)) for i in range(n_ctx) if par...  6.45 us
    pallas_call x1, Pallas kernels, local(): pl.pallas_call(lambda *refs: main_kernel(2 * n_ctx, doc_lengths.shape[0],...  6.09 us
    all_to_all x1, starting transfers between devices, exchange(): return lax.all_to_all(x, 'ctx', 0, 0, axis_index_groups=members, tiled=True)  4.47 us
  transfers between devices with their start and end apart: 10, of which 7 were waited for; matrix products, arithmetic and copies ran while one was open for 0% of the time, Pallas kernels for 0%

profile of v2, /device:TPU:352, one launch (start us, length us, event | category | flops | bytes accessed | tf_op | source)
XLA Modules:
  0.0 110.7 jit_solution(1783331760307235177)
XLA Ops:
  0.0 1.7 %prep.1 = (bf16[256,128]{1,0:T(8,128)(2,1)S(1)}, bf16[256,128]{1,0:T(8,128)(2,1)S(1)}, bf16[8,256,128]{2,1,0:T(8,128)(2,1)}) custom-call(bf16[256,128]{1,0:T(8,128)(2,1)} %refs_1_.1, bf16[256,128]{1,0:T(8,128)(2,1)} %refs_2_.1), custom_call_target="tpu_custom_call" | custom-call | tf_op jit(solution)/shard_map/prep/pallas_call | solution.py:155
  1.7 4.5 %all-to-all-start = ((bf16[8,256,128]{2,1,0:T(8,128)(2,1)}), bf16[8,256,128]{2,1,0:T(8,128)(2,1)S(1)}, u32[]{:S(2)}, u32[]{:S(2)}) async-start(bf16[8,256,128]{2,1,0:T(8,128)(2,1)} %get-tuple-element.16), calls=%async_computation | async-start | bytes 1048576 | tf_op jit(solution)/shard_map/all_to_all | solution.py:173
  6.2 3.4 %collective-permute-start = (bf16[256,128]{1,0:T(8,128)(2,1)S(1)}, bf16[256,128]{1,0:T(8,128)(2,1)S(1)}, u32[]{:S(2)}, u32[]{:S(2)}) collective-permute-start(bf16[256,128]{1,0:T(8,128)(2,1)S(1)} %get-tuple-element.17), channel_id=1, source_target_pairs={{0,64},{8,72},{16,80},{24,88},{32,96},{40,104},{48,112},{56,120},{... | collective-permute-start | bytes 196616 | tf_op jit(solution)/shard_map/ppermute | solution.py:166
  9.6 3.1 %collective-permute-start.1 = (bf16[256,128]{1,0:T(8,128)(2,1)S(1)}, bf16[256,128]{1,0:T(8,128)(2,1)S(1)}, u32[]{:S(2)}, u32[]{:S(2)}) collective-permute-start(bf16[256,128]{1,0:T(8,128)(2,1)S(1)} %get-tuple-element.18), channel_id=1, source_target_pairs={{64,128},{72,136},{80,144},{88,152},{96,160},{104,168},{112,176},{... | collective-permute-start | bytes 196616 | tf_op jit(solution)/shard_map/ppermute | solution.py:166
  12.7 0.0 collective-permute-done.even_ref
  12.7 16.8 %collective-permute-done.1.odd_ref = bf16[256,128]{1,0:T(8,128)(2,1)S(1)} collective-permute-done((bf16[256,128]{1,0:T(8,128)(2,1)S(1)}, bf16[256,128]{1,0:T(8,128)(2,1)S(1)}, u32[]{:S(2)}, u32[]{:S(2)}) %collective-permute-start.1) | collective-permute-done | bytes 65568 | tf_op jit(solution)/shard_map/ppermute | solution.py:166
  29.5 0.1 pass.1
  29.5 0.0 all-to-all-done.refs_3_
  29.6 0.0 copy-start
  29.6 14.7 %all_to_all.10.refs_4_ = bf16[8,256,128]{2,1,0:T(8,128)(2,1)S(1)} all-to-all(bf16[8,256,128]{2,1,0:T(8,128)(2,1)S(1)} %pass.1), channel_id=1, replica_groups={{0,8,16,24,32,40,48,56},{64,72,80,88,96,104,112,120},{128,136,144,152,1..., dimensions={0} | all-to-all | bytes 1048576 | tf_op jit(solution)/shard_map/all_to_all | solution.py:173
  44.2 0.0 copy-done
  44.2 6.1 %attend.1 = (bf16[32,4096]{1,0:T(8,128)(2,1)S(1)}, bf16[32,4096]{1,0:T(8,128)(2,1)S(1)}, bf16[32,4096]{1,0:T(8,128)(2,1)S(1)}, bf16[32,4096]{1,0:T(8,128)(2,1)S(...) custom-call(bf16[256,512]{1,0:T(8,128)(2,1)} %refs_0_.1, ...), custom_call_target="tpu_custom_call" | custom-call | tf_op jit(solution)/shard_map/attend/pallas_call | solution.py:184
  50.3 4.8 %collective-permute-start.2 = (bf16[32,4096]{1,0:T(8,128)(2,1)S(1)}, bf16[32,4096]{1,0:T(8,128)(2,1)S(1)}, u32[]{:S(2)}, u32[]{:S(2)}) collective-permute-start(bf16[32,4096]{1,0:T(8,128)(2,1)S(1)} %get-tuple-element.23), channel_id=1, source_target_pairs={{0,2},{2,4},{4,6},{6,7},{7,5},{5,3},{3,1},{1,0},{8,10},{10,12},{12... | collective-permute-start | bytes 786440 | tf_op jit(solution)/shard_map/ppermute | solution.py:211
  55.1 3.2 %collective-permute-start.6 = (bf16[32,4096]{1,0:T(8,128)(2,1)S(1)}, bf16[32,4096]{1,0:T(8,128)(2,1)S(1)}, u32[]{:S(2)}, u32[]{:S(2)}) collective-permute-start(bf16[32,4096]{1,0:T(8,128)(2,1)S(1)} %get-tuple-element.26), channel_id=1, source_target_pairs={{2,0},{4,2},{6,4},{7,6},{5,7},{3,5},{1,3},{0,1},{10,8},{12,10},{14... | collective-permute-start | bytes 786440 | tf_op jit(solution)/shard_map/ppermute | solution.py:213
  58.3 9.4 %collective-permute-done.2 = bf16[32,4096]{1,0:T(8,128)(2,1)S(1)} collective-permute-done((bf16[32,4096]{1,0:T(8,128)(2,1)S(1)}, bf16[32,4096]{1,0:T(8,128)(2,1)S(1)}, u32[]{:S(2)}, u32[]{:S(2)}) %collective-permute-start.2) | collective-permute-done | bytes 262176 | tf_op jit(solution)/shard_map/ppermute | solution.py:211
  67.7 0.1 add_convert_fusion.5
  67.7 3.6 %collective-permute-start.3 = (bf16[32,4096]{1,0:T(8,128)(2,1)S(1)}, bf16[32,4096]{1,0:T(8,128)(2,1)S(1)}, u32[]{:S(2)}, u32[]{:S(2)}) collective-permute-start(bf16[32,4096]{1,0:T(8,128)(2,1)S(1)} %add_convert_fusion.5), channel_id=1, source_target_pairs={{0,2},{2,4},{4,6},{6,7},{7,5},{5,3},{3,1},{1,0},{8,10},{10,12},{12... | collective-permute-start | bytes 786440 | tf_op jit(solution)/shard_map/ppermute | solution.py:211
  71.3 0.4 collective-permute-done.6
  71.7 0.1 add_convert_fusion.2
  71.7 4.0 %collective-permute-start.7 = (bf16[32,4096]{1,0:T(8,128)(2,1)S(1)}, bf16[32,4096]{1,0:T(8,128)(2,1)S(1)}, u32[]{:S(2)}, u32[]{:S(2)}) collective-permute-start(bf16[32,4096]{1,0:T(8,128)(2,1)S(1)} %add_convert_fusion.2), channel_id=1, source_target_pairs={{2,0},{4,2},{6,4},{7,6},{5,7},{3,5},{1,3},{0,1},{10,8},{12,10},{14... | collective-permute-start | bytes 786440 | tf_op jit(solution)/shard_map/ppermute | solution.py:213
  75.8 6.6 %collective-permute-done.3 = bf16[32,4096]{1,0:T(8,128)(2,1)S(1)} collective-permute-done((bf16[32,4096]{1,0:T(8,128)(2,1)S(1)}, bf16[32,4096]{1,0:T(8,128)(2,1)S(1)}, u32[]{:S(2)}, u32[]{:S(2)}) %collective-permute-start.3) | collective-permute-done | bytes 262176 | tf_op jit(solution)/shard_map/ppermute | solution.py:211
  82.4 0.1 add_convert_fusion.4
  82.5 1.9 %collective-permute-start.4 = (bf16[32,4096]{1,0:T(8,128)(2,1)S(1)}, bf16[32,4096]{1,0:T(8,128)(2,1)S(1)}, u32[]{:S(2)}, u32[]{:S(2)}) collective-permute-start(bf16[32,4096]{1,0:T(8,128)(2,1)S(1)} %add_convert_fusion.4), channel_id=1, source_target_pairs={{0,2},{2,4},{4,6},{6,7},{7,5},{5,3},{3,1},{1,0},{8,10},{10,12},{12... | collective-permute-start | bytes 786440 | tf_op jit(solution)/shard_map/ppermute | solution.py:211
  84.4 1.1 collective-permute-done.7
  85.5 0.1 add_convert_fusion.1
  85.6 6.5 %collective-permute-start.8 = (bf16[32,4096]{1,0:T(8,128)(2,1)S(1)}, bf16[32,4096]{1,0:T(8,128)(2,1)S(1)}, u32[]{:S(2)}, u32[]{:S(2)}) collective-permute-start(bf16[32,4096]{1,0:T(8,128)(2,1)S(1)} %add_convert_fusion.1), channel_id=1, source_target_pairs={{2,0},{4,2},{6,4},{7,6},{5,7},{3,5},{1,3},{0,1},{10,8},{12,10},{14... | collective-permute-start | bytes 786440 | tf_op jit(solution)/shard_map/ppermute | solution.py:213
  92.0 7.3 %collective-permute-done.4 = bf16[32,4096]{1,0:T(8,128)(2,1)S(1)} collective-permute-done((bf16[32,4096]{1,0:T(8,128)(2,1)S(1)}, bf16[32,4096]{1,0:T(8,128)(2,1)S(1)}, u32[]{:S(2)}, u32[]{:S(2)}) %collective-permute-start.4) | collective-permute-done | bytes 262176 | tf_op jit(solution)/shard_map/ppermute | solution.py:211
  99.3 0.1 add_convert_fusion.3
  99.4 1.9 %collective-permute-start.5 = (bf16[32,4096]{1,0:T(8,128)(2,1)S(1)}, bf16[32,4096]{1,0:T(8,128)(2,1)S(1)}, u32[]{:S(2)}, u32[]{:S(2)}) collective-permute-start(bf16[32,4096]{1,0:T(8,128)(2,1)S(1)} %add_convert_fusion.3), channel_id=1, source_target_pairs={{0,2},{2,4},{4,6},{6,7},{7,5},{5,3},{3,1},{1,0},{8,10},{10,12},{12... | collective-permute-start | bytes 786440 | tf_op jit(solution)/shard_map/ppermute | solution.py:211
  101.3 0.0 collective-permute-done.8
  101.3 8.6 %collective-permute-done.5 = bf16[32,4096]{1,0:T(8,128)(2,1)S(1)} collective-permute-done((bf16[32,4096]{1,0:T(8,128)(2,1)S(1)}, bf16[32,4096]{1,0:T(8,128)(2,1)S(1)}, u32[]{:S(2)}, u32[]{:S(2)}) %collective-permute-start.5) | collective-permute-done | bytes 262176 | tf_op jit(solution)/shard_map/ppermute | solution.py:211
  109.9 0.8 add_convert_fusion
Async XLA Ops:
  1.7 27.8 %all-to-all-start = ((bf16[8,256,128]{2,1,0:T(8,128)(2,1)}), bf16[8,256,128]{2,1,0:T(8,128)(2,1)S(1)}, u32[]{:S(2)}, u32[]{:S(2)}) async-start(bf16[8,256,128]{2,1,0:T(8,128)(2,1)} %get-tuple-element.16), calls=%async_computation | async-start | bytes 1048576 | tf_op jit(solution)/shard_map/all_to_all | solution.py:173
  6.2 6.5 %collective-permute-start = (bf16[256,128]{1,0:T(8,128)(2,1)S(1)}, bf16[256,128]{1,0:T(8,128)(2,1)S(1)}, u32[]{:S(2)}, u32[]{:S(2)}) collective-permute-start(bf16[256,128]{1,0:T(8,128)(2,1)S(1)} %get-tuple-element.17), channel_id=1, source_target_pairs={{0,64},{8,72},{16,80},{24,88},{32,96},{40,104},{48,112},{56,120},{... | collective-permute-start | bytes 196616 | tf_op jit(solution)/shard_map/ppermute | solution.py:166
  9.6 19.9 %collective-permute-start.1 = (bf16[256,128]{1,0:T(8,128)(2,1)S(1)}, bf16[256,128]{1,0:T(8,128)(2,1)S(1)}, u32[]{:S(2)}, u32[]{:S(2)}) collective-permute-start(bf16[256,128]{1,0:T(8,128)(2,1)S(1)} %get-tuple-element.18), channel_id=1, source_target_pairs={{64,128},{72,136},{80,144},{88,152},{96,160},{104,168},{112,176},{... | collective-permute-start | bytes 196616 | tf_op jit(solution)/shard_map/ppermute | solution.py:166
  29.6 14.7 %copy-start = (bf16[8,256,128]{2,1,0:T(8,128)(2,1)}, bf16[8,256,128]{2,1,0:T(8,128)(2,1)S(1)}, u32[]{:S(2)}) copy-start(bf16[8,256,128]{2,1,0:T(8,128)(2,1)S(1)} %all-to-all-done.refs_3_) | copy-start | bytes 1572868
  50.3 17.3 %collective-permute-start.2 = (bf16[32,4096]{1,0:T(8,128)(2,1)S(1)}, bf16[32,4096]{1,0:T(8,128)(2,1)S(1)}, u32[]{:S(2)}, u32[]{:S(2)}) collective-permute-start(bf16[32,4096]{1,0:T(8,128)(2,1)S(1)} %get-tuple-element.23), channel_id=1, source_target_pairs={{0,2},{2,4},{4,6},{6,7},{7,5},{5,3},{3,1},{1,0},{8,10},{10,12},{12... | collective-permute-start | bytes 786440 | tf_op jit(solution)/shard_map/ppermute | solution.py:211
  55.1 16.5 %collective-permute-start.6 = (bf16[32,4096]{1,0:T(8,128)(2,1)S(1)}, bf16[32,4096]{1,0:T(8,128)(2,1)S(1)}, u32[]{:S(2)}, u32[]{:S(2)}) collective-permute-start(bf16[32,4096]{1,0:T(8,128)(2,1)S(1)} %get-tuple-element.26), channel_id=1, source_target_pairs={{2,0},{4,2},{6,4},{7,6},{5,7},{3,5},{1,3},{0,1},{10,8},{12,10},{14... | collective-permute-start | bytes 786440 | tf_op jit(solution)/shard_map/ppermute | solution.py:213
  67.7 14.7 %collective-permute-start.3 = (bf16[32,4096]{1,0:T(8,128)(2,1)S(1)}, bf16[32,4096]{1,0:T(8,128)(2,1)S(1)}, u32[]{:S(2)}, u32[]{:S(2)}) collective-permute-start(bf16[32,4096]{1,0:T(8,128)(2,1)S(1)} %add_convert_fusion.5), channel_id=1, source_target_pairs={{0,2},{2,4},{4,6},{6,7},{7,5},{5,3},{3,1},{1,0},{8,10},{10,12},{12... | collective-permute-start | bytes 786440 | tf_op jit(solution)/shard_map/ppermute | solution.py:211
  71.7 13.8 %collective-permute-start.7 = (bf16[32,4096]{1,0:T(8,128)(2,1)S(1)}, bf16[32,4096]{1,0:T(8,128)(2,1)S(1)}, u32[]{:S(2)}, u32[]{:S(2)}) collective-permute-start(bf16[32,4096]{1,0:T(8,128)(2,1)S(1)} %add_convert_fusion.2), channel_id=1, source_target_pairs={{2,0},{4,2},{6,4},{7,6},{5,7},{3,5},{1,3},{0,1},{10,8},{12,10},{14... | collective-permute-start | bytes 786440 | tf_op jit(solution)/shard_map/ppermute | solution.py:213
  82.5 16.8 %collective-permute-start.4 = (bf16[32,4096]{1,0:T(8,128)(2,1)S(1)}, bf16[32,4096]{1,0:T(8,128)(2,1)S(1)}, u32[]{:S(2)}, u32[]{:S(2)}) collective-permute-start(bf16[32,4096]{1,0:T(8,128)(2,1)S(1)} %add_convert_fusion.4), channel_id=1, source_target_pairs={{0,2},{2,4},{4,6},{6,7},{7,5},{5,3},{3,1},{1,0},{8,10},{10,12},{12... | collective-permute-start | bytes 786440 | tf_op jit(solution)/shard_map/ppermute | solution.py:211
  85.6 15.8 %collective-permute-start.8 = (bf16[32,4096]{1,0:T(8,128)(2,1)S(1)}, bf16[32,4096]{1,0:T(8,128)(2,1)S(1)}, u32[]{:S(2)}, u32[]{:S(2)}) collective-permute-start(bf16[32,4096]{1,0:T(8,128)(2,1)S(1)} %add_convert_fusion.1), channel_id=1, source_target_pairs={{2,0},{4,2},{6,4},{7,6},{5,7},{3,5},{1,3},{0,1},{10,8},{12,10},{14... | collective-permute-start | bytes 786440 | tf_op jit(solution)/shard_map/ppermute | solution.py:213
  99.4 10.5 %collective-permute-start.5 = (bf16[32,4096]{1,0:T(8,128)(2,1)S(1)}, bf16[32,4096]{1,0:T(8,128)(2,1)S(1)}, u32[]{:S(2)}, u32[]{:S(2)}) collective-permute-start(bf16[32,4096]{1,0:T(8,128)(2,1)S(1)} %add_convert_fusion.3), channel_id=1, source_target_pairs={{0,2},{2,4},{4,6},{6,7},{7,5},{5,3},{3,1},{1,0},{8,10},{10,12},{12... | collective-permute-start | bytes 786440 | tf_op jit(solution)/shard_map/ppermute | solution.py:211

commit v3 on v2

--- a/solution.py
+++ b/solution.py
@@ -13,6 +13,8 @@
 HEAD_WIDTH = 128
 STRETCH = 128
 GROUP = 8
+PAIR = 2
+TILE = 512
 NEG_FILL = -1e30
 SCALE = math.log2(math.e) / math.sqrt(HEAD_WIDTH)
 VMEM = pl.BlockSpec(memory_space=pltpu.VMEM)
@@ -66,7 +68,7 @@
 
 
 def main_kernel(stretches, docs, q_ref, k_ref, v_ref, own_ref, sh_ref, len_ref, w_hbm, *rest):
-    outs, (kbuf, vbuf, bias, attn, rows, wbuf, sem) = rest[:8], rest[8:]
+    outs, (kbuf, vbuf, bias, attn, rows, wbuf, sem) = rest[:-7], rest[-7:]
     ctx = lax.axis_index("ctx")
     kvh = lax.axis_index("kvh")
     me = lax.rem(ctx, GROUP)
@@ -115,17 +117,19 @@
             allowed = (key_place >= begin) & (key_place <= q_place)
             bias[:, here] = jnp.where(allowed, 0.0, NEG_FILL)
         mine = pl.ds(chain * STRETCH, STRETCH)
-        for h in range(heads):
-            columns = pl.ds(h * HEAD_WIDTH, HEAD_WIDTH)
-            scores = lax.dot_general(
-                q_ref[mine, columns], kbuf[...], (((1,), (1,)), ((), ())), preferred_element_type=F32
-            )
-            scores = scores * SCALE + bias[...]
-            highest = jnp.max(scores, axis=1, keepdims=True)
+        stack = jnp.concatenate([q_ref[mine, h * HEAD_WIDTH : (h + 1) * HEAD_WIDTH] for h in range(heads)], axis=0)
+        for g in range(0, heads, PAIR):
+            many = stack[g * STRETCH : (g + PAIR) * STRETCH]
+            scores = lax.dot_general(many, kbuf[...], (((1,), (1,)), ((), ())), preferred_element_type=F32)
+            scores = scores.reshape(PAIR, STRETCH, GROUP * STRETCH) * SCALE + bias[...][None]
+            highest = jnp.max(scores, axis=2, keepdims=True)
             weights = jnp.exp2(scores - highest)
-            total = jnp.sum(weights, axis=1, keepdims=True)
-            result = jnp.dot(weights.astype(BF), vbuf[...], preferred_element_type=F32)
-            attn[mine, columns] = (result / total).astype(BF)
+            total = jnp.sum(weights, axis=2, keepdims=True)
+            flat = weights.astype(BF).reshape(PAIR * STRETCH, GROUP * STRETCH)
+            result = jnp.dot(flat, vbuf[...], preferred_element_type=F32).reshape(PAIR, STRETCH, HEAD_WIDTH)
+            result = (result / total).astype(BF)
+            for h in range(PAIR):
+                attn[mine, (g + h) * HEAD_WIDTH : (g + h + 1) * HEAD_WIDTH] = result[h]
     n_kvh = len(outs)
     chunk = attn.shape[0] // n_kvh
     position = jnp.where(lax.rem(kvh, 2) == 0, kvh // 2, n_kvh - 1 - kvh // 2)
@@ -134,9 +138,8 @@
         to = jnp.where(i < n_kvh // 2, 2 * i, 2 * n_kvh - 1 - 2 * i)
         rows[pl.ds(o * chunk, chunk)] = attn[pl.ds(pl.multiple_of(to * chunk, chunk), chunk)]
     copy.wait()
-    width = 512
-    for c in range(wbuf.shape[1] // width):
-        columns = pl.ds(c * width, width)
+    for c in range(0, wbuf.shape[1], TILE):
+        columns = pl.ds(c, TILE)
         part = jnp.dot(rows[...], wbuf[:, columns], preferred_element_type=F32).astype(BF)
         for o in range(n_kvh):
             outs[o][:, columns] = part[o * chunk : (o + 1) * chunk]

time: 111 us -> 110 us (level)
  no operation moved by 1% of the time
where the time goes in v3:
time: 110 us
  waiting for transfers between devices  50 us (45%)
  starting transfers between devices  36.8 us (33%)
  blocking collectives  14.7 us (13%)
  Pallas kernels  7.08 us (6%)
  other arithmetic  1.12 us (1%)
    ppermute x4, waiting for transfers between devices, local(): a = lax.ppermute(a, 'kvh', onward)  31.8 us
    ppermute x2, waiting for transfers between devices, swap(): lax.ppermute(x, 'ctx', [(i, partner(i, odd)) for i in range(n_ctx) if par...  16.8 us
    all_to_all x1, blocking collectives, exchange(): return lax.all_to_all(x, 'ctx', 0, 0, axis_index_groups=members, tiled=True)  14.7 us
    ppermute x3, starting transfers between devices, local(): b = lax.ppermute(b, 'kvh', back)  13.7 us
    ppermute x4, starting transfers between devices, local(): a = lax.ppermute(a, 'kvh', onward)  12.2 us
    ppermute x2, starting transfers between devices, swap(): lax.ppermute(x, 'ctx', [(i, partner(i, odd)) for i in range(n_ctx) if par...  6.45 us
    pallas_call x1, Pallas kernels, local(): pl.pallas_call(lambda *refs: main_kernel(2 * n_ctx, doc_lengths.shape[0],...  5.26 us
    all_to_all x1, starting transfers between devices, exchange(): return lax.all_to_all(x, 'ctx', 0, 0, axis_index_groups=members, tiled=True)  4.47 us
  transfers between devices with their start and end apart: 10, of which 7 were waited for; matrix products, arithmetic and copies ran while one was open for 0% of the time, Pallas kernels for 0%

profile of v3, /device:TPU:352, one launch (start us, length us, event | category | flops | bytes accessed | tf_op | source)
XLA Modules:
  0.0 109.8 jit_solution(12801585525969356520)
XLA Ops:
  0.0 1.7 %prep.1 = (bf16[256,128]{1,0:T(8,128)(2,1)S(1)}, bf16[256,128]{1,0:T(8,128)(2,1)S(1)}, bf16[8,256,128]{2,1,0:T(8,128)(2,1)}) custom-call(bf16[256,128]{1,0:T(8,128)(2,1)} %refs_1_.1, bf16[256,128]{1,0:T(8,128)(2,1)} %refs_2_.1), custom_call_target="tpu_custom_call" | custom-call | tf_op jit(solution)/shard_map/prep/pallas_call | solution.py:158
  1.7 4.5 %all-to-all-start = ((bf16[8,256,128]{2,1,0:T(8,128)(2,1)}), bf16[8,256,128]{2,1,0:T(8,128)(2,1)S(1)}, u32[]{:S(2)}, u32[]{:S(2)}) async-start(bf16[8,256,128]{2,1,0:T(8,128)(2,1)} %get-tuple-element.16), calls=%async_computation | async-start | bytes 1048576 | tf_op jit(solution)/shard_map/all_to_all | solution.py:176
  6.2 3.4 %collective-permute-start = (bf16[256,128]{1,0:T(8,128)(2,1)S(1)}, bf16[256,128]{1,0:T(8,128)(2,1)S(1)}, u32[]{:S(2)}, u32[]{:S(2)}) collective-permute-start(bf16[256,128]{1,0:T(8,128)(2,1)S(1)} %get-tuple-element.17), channel_id=1, source_target_pairs={{0,64},{8,72},{16,80},{24,88},{32,96},{40,104},{48,112},{56,120},{... | collective-permute-start | bytes 196616 | tf_op jit(solution)/shard_map/ppermute | solution.py:169
  9.6 3.1 %collective-permute-start.1 = (bf16[256,128]{1,0:T(8,128)(2,1)S(1)}, bf16[256,128]{1,0:T(8,128)(2,1)S(1)}, u32[]{:S(2)}, u32[]{:S(2)}) collective-permute-start(bf16[256,128]{1,0:T(8,128)(2,1)S(1)} %get-tuple-element.18), channel_id=1, source_target_pairs={{64,128},{72,136},{80,144},{88,152},{96,160},{104,168},{112,176},{... | collective-permute-start | bytes 196616 | tf_op jit(solution)/shard_map/ppermute | solution.py:169
  12.7 0.0 collective-permute-done.even_ref
  12.7 16.8 %collective-permute-done.1.odd_ref = bf16[256,128]{1,0:T(8,128)(2,1)S(1)} collective-permute-done((bf16[256,128]{1,0:T(8,128)(2,1)S(1)}, bf16[256,128]{1,0:T(8,128)(2,1)S(1)}, u32[]{:S(2)}, u32[]{:S(2)}) %collective-permute-start.1) | collective-permute-done | bytes 65568 | tf_op jit(solution)/shard_map/ppermute | solution.py:169
  29.5 0.1 pass.1
  29.5 0.0 all-to-all-done.refs_3_
  29.6 0.0 copy-start
  29.6 14.7 %all_to_all.10.refs_4_ = bf16[8,256,128]{2,1,0:T(8,128)(2,1)S(1)} all-to-all(bf16[8,256,128]{2,1,0:T(8,128)(2,1)S(1)} %pass.1), channel_id=1, replica_groups={{0,8,16,24,32,40,48,56},{64,72,80,88,96,104,112,120},{128,136,144,152,1..., dimensions={0} | all-to-all | bytes 1048576 | tf_op jit(solution)/shard_map/all_to_all | solution.py:176
  44.2 0.0 copy-done
  44.2 5.3 %attend.1 = (bf16[32,4096]{1,0:T(8,128)(2,1)S(1)}, bf16[32,4096]{1,0:T(8,128)(2,1)S(1)}, bf16[32,4096]{1,0:T(8,128)(2,1)S(1)}, bf16[32,4096]{1,0:T(8,128)(2,1)S(...) custom-call(bf16[256,512]{1,0:T(8,128)(2,1)} %refs_0_.1, ...), custom_call_target="tpu_custom_call" | custom-call | tf_op jit(solution)/shard_map/attend/pallas_call | solution.py:187
  49.5 4.8 %collective-permute-start.2 = (bf16[32,4096]{1,0:T(8,128)(2,1)S(1)}, bf16[32,4096]{1,0:T(8,128)(2,1)S(1)}, u32[]{:S(2)}, u32[]{:S(2)}) collective-permute-start(bf16[32,4096]{1,0:T(8,128)(2,1)S(1)} %get-tuple-element.23), channel_id=1, source_target_pairs={{0,2},{2,4},{4,6},{6,7},{7,5},{5,3},{3,1},{1,0},{8,10},{10,12},{12... | collective-permute-start | bytes 786440 | tf_op jit(solution)/shard_map/ppermute | solution.py:214
  54.3 3.2 %collective-permute-start.6 = (bf16[32,4096]{1,0:T(8,128)(2,1)S(1)}, bf16[32,4096]{1,0:T(8,128)(2,1)S(1)}, u32[]{:S(2)}, u32[]{:S(2)}) collective-permute-start(bf16[32,4096]{1,0:T(8,128)(2,1)S(1)} %get-tuple-element.26), channel_id=1, source_target_pairs={{2,0},{4,2},{6,4},{7,6},{5,7},{3,5},{1,3},{0,1},{10,8},{12,10},{14... | collective-permute-start | bytes 786440 | tf_op jit(solution)/shard_map/ppermute | solution.py:216
  57.5 9.3 %collective-permute-done.2 = bf16[32,4096]{1,0:T(8,128)(2,1)S(1)} collective-permute-done((bf16[32,4096]{1,0:T(8,128)(2,1)S(1)}, bf16[32,4096]{1,0:T(8,128)(2,1)S(1)}, u32[]{:S(2)}, u32[]{:S(2)}) %collective-permute-start.2) | collective-permute-done | bytes 262176 | tf_op jit(solution)/shard_map/ppermute | solution.py:214
  66.8 0.1 add_convert_fusion.5
  66.9 3.6 %collective-permute-start.3 = (bf16[32,4096]{1,0:T(8,128)(2,1)S(1)}, bf16[32,4096]{1,0:T(8,128)(2,1)S(1)}, u32[]{:S(2)}, u32[]{:S(2)}) collective-permute-start(bf16[32,4096]{1,0:T(8,128)(2,1)S(1)} %add_convert_fusion.5), channel_id=1, source_target_pairs={{0,2},{2,4},{4,6},{6,7},{7,5},{5,3},{3,1},{1,0},{8,10},{10,12},{12... | collective-permute-start | bytes 786440 | tf_op jit(solution)/shard_map/ppermute | solution.py:214
  70.5 0.4 collective-permute-done.6
  70.8 0.1 add_convert_fusion.2
  70.9 4.0 %collective-permute-start.7 = (bf16[32,4096]{1,0:T(8,128)(2,1)S(1)}, bf16[32,4096]{1,0:T(8,128)(2,1)S(1)}, u32[]{:S(2)}, u32[]{:S(2)}) collective-permute-start(bf16[32,4096]{1,0:T(8,128)(2,1)S(1)} %add_convert_fusion.2), channel_id=1, source_target_pairs={{2,0},{4,2},{6,4},{7,6},{5,7},{3,5},{1,3},{0,1},{10,8},{12,10},{14... | collective-permute-start | bytes 786440 | tf_op jit(solution)/shard_map/ppermute | solution.py:216
  74.9 6.6 %collective-permute-done.3 = bf16[32,4096]{1,0:T(8,128)(2,1)S(1)} collective-permute-done((bf16[32,4096]{1,0:T(8,128)(2,1)S(1)}, bf16[32,4096]{1,0:T(8,128)(2,1)S(1)}, u32[]{:S(2)}, u32[]{:S(2)}) %collective-permute-start.3) | collective-permute-done | bytes 262176 | tf_op jit(solution)/shard_map/ppermute | solution.py:214
  81.6 0.1 add_convert_fusion.4
  81.6 1.9 %collective-permute-start.4 = (bf16[32,4096]{1,0:T(8,128)(2,1)S(1)}, bf16[32,4096]{1,0:T(8,128)(2,1)S(1)}, u32[]{:S(2)}, u32[]{:S(2)}) collective-permute-start(bf16[32,4096]{1,0:T(8,128)(2,1)S(1)} %add_convert_fusion.4), channel_id=1, source_target_pairs={{0,2},{2,4},{4,6},{6,7},{7,5},{5,3},{3,1},{1,0},{8,10},{10,12},{12... | collective-permute-start | bytes 786440 | tf_op jit(solution)/shard_map/ppermute | solution.py:214
  83.6 1.1 collective-permute-done.7
  84.6 0.1 add_convert_fusion.1
  84.7 6.5 %collective-permute-start.8 = (bf16[32,4096]{1,0:T(8,128)(2,1)S(1)}, bf16[32,4096]{1,0:T(8,128)(2,1)S(1)}, u32[]{:S(2)}, u32[]{:S(2)}) collective-permute-start(bf16[32,4096]{1,0:T(8,128)(2,1)S(1)} %add_convert_fusion.1), channel_id=1, source_target_pairs={{2,0},{4,2},{6,4},{7,6},{5,7},{3,5},{1,3},{0,1},{10,8},{12,10},{14... | collective-permute-start | bytes 786440 | tf_op jit(solution)/shard_map/ppermute | solution.py:216
  91.2 7.3 %collective-permute-done.4 = bf16[32,4096]{1,0:T(8,128)(2,1)S(1)} collective-permute-done((bf16[32,4096]{1,0:T(8,128)(2,1)S(1)}, bf16[32,4096]{1,0:T(8,128)(2,1)S(1)}, u32[]{:S(2)}, u32[]{:S(2)}) %collective-permute-start.4) | collective-permute-done | bytes 262176 | tf_op jit(solution)/shard_map/ppermute | solution.py:214
  98.5 0.1 add_convert_fusion.3
  98.5 1.9 %collective-permute-start.5 = (bf16[32,4096]{1,0:T(8,128)(2,1)S(1)}, bf16[32,4096]{1,0:T(8,128)(2,1)S(1)}, u32[]{:S(2)}, u32[]{:S(2)}) collective-permute-start(bf16[32,4096]{1,0:T(8,128)(2,1)S(1)} %add_convert_fusion.3), channel_id=1, source_target_pairs={{0,2},{2,4},{4,6},{6,7},{7,5},{5,3},{3,1},{1,0},{8,10},{10,12},{12... | collective-permute-start | bytes 786440 | tf_op jit(solution)/shard_map/ppermute | solution.py:214
  100.5 0.0 collective-permute-done.8
  100.5 8.6 %collective-permute-done.5 = bf16[32,4096]{1,0:T(8,128)(2,1)S(1)} collective-permute-done((bf16[32,4096]{1,0:T(8,128)(2,1)S(1)}, bf16[32,4096]{1,0:T(8,128)(2,1)S(1)}, u32[]{:S(2)}, u32[]{:S(2)}) %collective-permute-start.5) | collective-permute-done | bytes 262176 | tf_op jit(solution)/shard_map/ppermute | solution.py:214
  109.0 0.8 add_convert_fusion
Async XLA Ops:
  1.7 27.8 %all-to-all-start = ((bf16[8,256,128]{2,1,0:T(8,128)(2,1)}), bf16[8,256,128]{2,1,0:T(8,128)(2,1)S(1)}, u32[]{:S(2)}, u32[]{:S(2)}) async-start(bf16[8,256,128]{2,1,0:T(8,128)(2,1)} %get-tuple-element.16), calls=%async_computation | async-start | bytes 1048576 | tf_op jit(solution)/shard_map/all_to_all | solution.py:176
  6.2 6.5 %collective-permute-start = (bf16[256,128]{1,0:T(8,128)(2,1)S(1)}, bf16[256,128]{1,0:T(8,128)(2,1)S(1)}, u32[]{:S(2)}, u32[]{:S(2)}) collective-permute-start(bf16[256,128]{1,0:T(8,128)(2,1)S(1)} %get-tuple-element.17), channel_id=1, source_target_pairs={{0,64},{8,72},{16,80},{24,88},{32,96},{40,104},{48,112},{56,120},{... | collective-permute-start | bytes 196616 | tf_op jit(solution)/shard_map/ppermute | solution.py:169
  9.6 19.9 %collective-permute-start.1 = (bf16[256,128]{1,0:T(8,128)(2,1)S(1)}, bf16[256,128]{1,0:T(8,128)(2,1)S(1)}, u32[]{:S(2)}, u32[]{:S(2)}) collective-permute-start(bf16[256,128]{1,0:T(8,128)(2,1)S(1)} %get-tuple-element.18), channel_id=1, source_target_pairs={{64,128},{72,136},{80,144},{88,152},{96,160},{104,168},{112,176},{... | collective-permute-start | bytes 196616 | tf_op jit(solution)/shard_map/ppermute | solution.py:169
  29.6 14.7 %copy-start = (bf16[8,256,128]{2,1,0:T(8,128)(2,1)}, bf16[8,256,128]{2,1,0:T(8,128)(2,1)S(1)}, u32[]{:S(2)}) copy-start(bf16[8,256,128]{2,1,0:T(8,128)(2,1)S(1)} %all-to-all-done.refs_3_) | copy-start | bytes 1572868
  49.5 17.3 %collective-permute-start.2 = (bf16[32,4096]{1,0:T(8,128)(2,1)S(1)}, bf16[32,4096]{1,0:T(8,128)(2,1)S(1)}, u32[]{:S(2)}, u32[]{:S(2)}) collective-permute-start(bf16[32,4096]{1,0:T(8,128)(2,1)S(1)} %get-tuple-element.23), channel_id=1, source_target_pairs={{0,2},{2,4},{4,6},{6,7},{7,5},{5,3},{3,1},{1,0},{8,10},{10,12},{12... | collective-permute-start | bytes 786440 | tf_op jit(solution)/shard_map/ppermute | solution.py:214
  54.3 16.5 %collective-permute-start.6 = (bf16[32,4096]{1,0:T(8,128)(2,1)S(1)}, bf16[32,4096]{1,0:T(8,128)(2,1)S(1)}, u32[]{:S(2)}, u32[]{:S(2)}) collective-permute-start(bf16[32,4096]{1,0:T(8,128)(2,1)S(1)} %get-tuple-element.26), channel_id=1, source_target_pairs={{2,0},{4,2},{6,4},{7,6},{5,7},{3,5},{1,3},{0,1},{10,8},{12,10},{14... | collective-permute-start | bytes 786440 | tf_op jit(solution)/shard_map/ppermute | solution.py:216
  66.9 14.7 %collective-permute-start.3 = (bf16[32,4096]{1,0:T(8,128)(2,1)S(1)}, bf16[32,4096]{1,0:T(8,128)(2,1)S(1)}, u32[]{:S(2)}, u32[]{:S(2)}) collective-permute-start(bf16[32,4096]{1,0:T(8,128)(2,1)S(1)} %add_convert_fusion.5), channel_id=1, source_target_pairs={{0,2},{2,4},{4,6},{6,7},{7,5},{5,3},{3,1},{1,0},{8,10},{10,12},{12... | collective-permute-start | bytes 786440 | tf_op jit(solution)/shard_map/ppermute | solution.py:214
  70.9 13.7 %collective-permute-start.7 = (bf16[32,4096]{1,0:T(8,128)(2,1)S(1)}, bf16[32,4096]{1,0:T(8,128)(2,1)S(1)}, u32[]{:S(2)}, u32[]{:S(2)}) collective-permute-start(bf16[32,4096]{1,0:T(8,128)(2,1)S(1)} %add_convert_fusion.2), channel_id=1, source_target_pairs={{2,0},{4,2},{6,4},{7,6},{5,7},{3,5},{1,3},{0,1},{10,8},{12,10},{14... | collective-permute-start | bytes 786440 | tf_op jit(solution)/shard_map/ppermute | solution.py:216
  81.6 16.9 %collective-permute-start.4 = (bf16[32,4096]{1,0:T(8,128)(2,1)S(1)}, bf16[32,4096]{1,0:T(8,128)(2,1)S(1)}, u32[]{:S(2)}, u32[]{:S(2)}) collective-permute-start(bf16[32,4096]{1,0:T(8,128)(2,1)S(1)} %add_convert_fusion.4), channel_id=1, source_target_pairs={{0,2},{2,4},{4,6},{6,7},{7,5},{5,3},{3,1},{1,0},{8,10},{10,12},{12... | collective-permute-start | bytes 786440 | tf_op jit(solution)/shard_map/ppermute | solution.py:214
  84.7 15.8 %collective-permute-start.8 = (bf16[32,4096]{1,0:T(8,128)(2,1)S(1)}, bf16[32,4096]{1,0:T(8,128)(2,1)S(1)}, u32[]{:S(2)}, u32[]{:S(2)}) collective-permute-start(bf16[32,4096]{1,0:T(8,128)(2,1)S(1)} %add_convert_fusion.1), channel_id=1, source_target_pairs={{2,0},{4,2},{6,4},{7,6},{5,7},{3,5},{1,3},{0,1},{10,8},{12,10},{14... | collective-permute-start | bytes 786440 | tf_op jit(solution)/shard_map/ppermute | solution.py:216
  98.5 10.5 %collective-permute-start.5 = (bf16[32,4096]{1,0:T(8,128)(2,1)S(1)}, bf16[32,4096]{1,0:T(8,128)(2,1)S(1)}, u32[]{:S(2)}, u32[]{:S(2)}) collective-permute-start(bf16[32,4096]{1,0:T(8,128)(2,1)S(1)} %add_convert_fusion.3), channel_id=1, source_target_pairs={{0,2},{2,4},{4,6},{6,7},{7,5},{5,3},{3,1},{1,0},{8,10},{10,12},{12... | collective-permute-start | bytes 786440 | tf_op jit(solution)/shard_map/ppermute | solution.py:214
